TPU v7x, 256 devices: a whole 4x4x8 slice. The times are simulated.
256 devices in a mesh: row: 16 (over x, z_hi), col: 16 (over y, z_lo, core).
Axes of the slice: x: 4, y: 4, z: 8 (z_hi: 4, z_lo: 2; z = z_hi * 2 + z_lo), core: 2. Of those that a mesh axis runs over, the one named last changes fastest.
Arguments:
- object_field: float32 [2, 4096, 4096], P(None, 'row', 'col'), may hold values from -6 to 6
- probe: float32 [2, 4, 128, 128], replicated, may hold values from -3 to 3
- amplitudes: float32 [16, 16, 3, 4, 128, 128], P('row', 'col'), may hold values from 0.3 to 3
- offsets: int32 [16, 16, 3, 4, 2], P('row', 'col'), may hold values from -64 to 192, as said below
Outputs:
- object_new: float32 [2, 4096, 4096], P(None, 'row', 'col')
- probe_step: float32 [2, 4, 128, 128], replicated
Inputs may be any that keep to these rules, and one draw needn't show every extreme that they name: `offsets`: in every batch of every device the first position is at (-64, -64) and the second at (192, 192).
All inputs are finite; a program needn't handle non-finite values.
Results may differ from a plain program's by a relative error of at most 0.0001.
Values sent between devices are 32-bit elements; how exact they have to be, the bound alone decides.
A program may use at most 64 MiB of HBM per device.

v0:
```python
import math

import jax
import jax.numpy as jnp
from jax import lax
from jax.sharding import PartitionSpec as P

PATCH = 128
BATCHES = 3


AMP_FLOOR = 0.25
OBJECT_REG = 0.5
PROBE_REG = 1.0
PRECISE_DOT = lax.Precision.HIGHEST


def from_behind(block, axis, distance):
    devices = range(lax.axis_size(axis))
    route = [(i - distance, i) for i in devices if i - distance in devices]
    return lax.ppermute(block, axis, route)


def padded_2(value, sides, width):
    for axis, dim in sides:
        peers, length = (lax.axis_size(axis), value.shape[dim])
        up = [(i, (i + 1) % peers) for i in range(peers - 1)]
        down = [(j, i) for i, j in up]
        last = lax.slice_in_dim(value, length - width, length, axis=dim)
        first = lax.slice_in_dim(value, 0, width, axis=dim)
        before = lax.ppermute(last, axis, up)
        after = lax.ppermute(first, axis, down)
        value = jnp.concatenate([before, value, after], axis=dim)
    return value


def together(arrays, axis):
    flat, at, outs = (jnp.concatenate([a.reshape(-1) for a in arrays]), 0, [])
    subtotal = lax.psum(flat, axis)
    for a in arrays:
        outs.append(subtotal[at : at + a.size].reshape(a.shape))
        at += a.size
    return tuple(outs)


def dft_tables(length):
    indices = jnp.arange(length, dtype=jnp.int32)
    product = indices[:, None] * indices[None, :] % length
    angles = product.astype(jnp.float32) * (2.0 * math.pi / length)
    factor_norm = 1.0 / math.sqrt(length)
    return (jnp.cos(angles) * factor_norm, -jnp.sin(angles) * factor_norm)


def transform(field_real, field_imag, table_real, table_imag, direction):
    signed = direction * table_imag
    left_real = jnp.einsum(
        "jk,...kl->...jl", table_real, field_real, precision=PRECISE_DOT
    ) - jnp.einsum("jk,...kl->...jl", signed, field_imag, precision=PRECISE_DOT)
    left_imag = jnp.einsum(
        "jk,...kl->...jl", table_real, field_imag, precision=PRECISE_DOT
    ) + jnp.einsum("jk,...kl->...jl", signed, field_real, precision=PRECISE_DOT)
    out_real = jnp.einsum(
        "...jk,kl->...jl", left_real, table_real, precision=PRECISE_DOT
    ) - jnp.einsum("...jk,kl->...jl", left_imag, signed, precision=PRECISE_DOT)
    out_imag = jnp.einsum(
        "...jk,kl->...jl", left_imag, table_real, precision=PRECISE_DOT
    ) + jnp.einsum("...jk,kl->...jl", left_real, signed, precision=PRECISE_DOT)
    return (out_real, out_imag)


def patch_terms(patch_real, patch_imag, probe_real, probe_imag, measured, table_real, table_imag):
    wave_real = probe_real[None] * patch_real[:, None] - probe_imag[None] * patch_imag[:, None]
    wave_imag = probe_real[None] * patch_imag[:, None] + probe_imag[None] * patch_real[:, None]
    far_real, far_imag = transform(wave_real, wave_imag, table_real, table_imag, 1.0)
    intensity = jnp.sum(far_real * far_real + far_imag * far_imag, axis=1)
    factor = measured / jnp.maximum(jnp.sqrt(intensity), AMP_FLOOR) - 1.0
    change_real, change_imag = transform(
        factor[:, None] * far_real, factor[:, None] * far_imag, table_real, table_imag, -1.0
    )
    object_real = jnp.sum(probe_real[None] * change_real + probe_imag[None] * change_imag, axis=1)
    object_imag = jnp.sum(probe_real[None] * change_imag - probe_imag[None] * change_real, axis=1)
    gradient_real = jnp.sum(
        patch_real[:, None] * change_real + patch_imag[:, None] * change_imag, axis=0
    )
    gradient_imag = jnp.sum(
        patch_real[:, None] * change_imag - patch_imag[:, None] * change_real, axis=0
    )
    object_power = jnp.sum(patch_real * patch_real + patch_imag * patch_imag, axis=0)
    return (object_real, object_imag, gradient_real, gradient_imag, object_power)


def cut_patches(padded, row_starts, col_starts, length):
    zero_start = jnp.zeros((), jnp.int32)

    def one_patch(row_start, col_start):
        return lax.dynamic_slice(padded, (zero_start, row_start, col_start), (2, length, length))

    return jax.vmap(one_patch)(row_starts, col_starts)


def scatter_patches(buffer, stacked, row_starts, col_starts, length):
    zero_start = jnp.zeros((), jnp.int32)

    def add_patch(position, current):
        corner = (zero_start, row_starts[position], col_starts[position])
        region = lax.dynamic_slice(current, corner, (3, length, length))
        return lax.dynamic_update_slice(current, region + stacked[position], corner)

    return lax.fori_loop(0, stacked.shape[0], add_patch, buffer)


def owner_totals(buffer, half_patch):
    top_rows = buffer[:, :half_patch]
    bottom_rows = buffer[:, -half_patch:]
    from_above = from_behind(bottom_rows, "row", 1)
    from_below = from_behind(top_rows, "row", -1)
    middle = buffer[:, half_patch:-half_patch]
    middle = middle.at[:, :half_patch].add(from_above).at[:, -half_patch:].add(from_below)
    left_cols = middle[:, :, :half_patch]
    right_cols = middle[:, :, -half_patch:]
    from_left = from_behind(right_cols, "col", 1)
    from_right = from_behind(left_cols, "col", -1)
    center = middle[:, :, half_patch:-half_patch]
    return center.at[:, :, :half_patch].add(from_left).at[:, :, -half_patch:].add(from_right)


def on_device(object_field, probe, amplitudes, offsets):
    half_patch = PATCH // 2
    tile_rows = object_field.shape[1]
    tile_cols = object_field.shape[2]
    table_real, table_imag = dft_tables(PATCH)
    probe_real, probe_imag = (probe[0], probe[1])
    lighting = jnp.sum(probe_real * probe_real + probe_imag * probe_imag, axis=0)
    grad_real = jnp.zeros(probe_real.shape, jnp.float32)
    grad_imag = jnp.zeros(probe_real.shape, jnp.float32)
    power_total = jnp.zeros((PATCH, PATCH), jnp.float32)
    current_object = object_field
    for batch_index in range(BATCHES):
        padded = padded_2(current_object, (("row", 1), ("col", 2)), half_patch)
        row_starts = offsets[0, 0, batch_index, :, 0] + half_patch
        col_starts = offsets[0, 0, batch_index, :, 1] + half_patch
        patches = cut_patches(padded, row_starts, col_starts, PATCH)
        object_real, object_imag, batch_real, batch_imag, batch_power = patch_terms(
            patches[:, 0],
            patches[:, 1],
            probe_real,
            probe_imag,
            amplitudes[0, 0, batch_index],
            table_real,
            table_imag,
        )
        stacked = jnp.stack(
            [object_real, object_imag, jnp.broadcast_to(lighting, object_real.shape)], axis=1
        )
        buffer = jnp.zeros((3, tile_rows + PATCH, tile_cols + PATCH), jnp.float32)
        buffer = scatter_patches(buffer, stacked, row_starts, col_starts, PATCH)
        totals = owner_totals(buffer, half_patch)
        current_object = current_object + totals[0:2] / (totals[2] + OBJECT_REG)
        grad_real = grad_real + batch_real
        grad_imag = grad_imag + batch_imag
        power_total = power_total + batch_power
    grad_real, grad_imag, power_total = together(
        (grad_real, grad_imag, power_total), ("row", "col")
    )
    root_power = jnp.sqrt(power_total + PROBE_REG)
    probe_step = jnp.stack([grad_real / root_power, grad_imag / root_power])
    return (current_object, probe_step)


def solution(mesh):
    placed = (
        P(None, "row", "col"),
        P(),
        P("row", "col", None, None, None, None),
        P("row", "col", None, None, None),
    )
    return jax.shard_map(
        on_device,
        mesh=mesh,
        in_specs=placed,
        out_specs=(P(None, "row", "col"), P()),
        check_vma=False,
    )
```

profile of v0, /device:TPU:1, one launch (start us, length us, event | category | flops | bytes accessed | tf_op | source)
XLA Modules:
  0.0 699.8 jit_solution(15282509463175756219)
XLA Ops:
  8.3 5.7 collective-permute-start
  17.5 9.0 %collective-permute-done.1 = f32[2,64,256]{2,1,0:T(8,128)S(1)} collective-permute-done((f32[2,64,256]{2,1,0:T(8,128)S(1)}, f32[2,64,256]{2,1,0:T(8,128)S(1)}, u32[]{:S(2)}, u32[]{:S(2)}) %collective-permute-start.1) | collective-permute-done | bytes 131104 | tf_op jit(solution)/shard_map/ppermute | solution.py:32
  33.3 8.0 %collective-permute-done.3 = f32[2,384,64]{2,1,0:T(8,128)S(1)} collective-permute-done((f32[2,384,64]{2,1,0:T(8,128)S(1)}, f32[2,384,64]{2,1,0:T(8,128)S(1)}, u32[]{:S(2)}, u32[]{:S(2)}) %collective-permute-start.3) | collective-permute-done | bytes 196640 | tf_op jit(solution)/shard_map/ppermute | solution.py:32
  41.7 8.3 %while.57 = (s32[]{:T(128)}, f32[2,384,384]{2,1,0:T(8,128)S(1)}, s32[4,3]{1,0:T(4,128)S(1)}, f32[4,2,128,128]{3,2,1,0:T(8,128)S(1)}, s32[]{:T(128)}) while((s32[]{:T(128)}, f32[2,384,384]{2,1,0:T(8,128)S(1)}, s32[4,3]{1,0:T(4,128)S(1)}, f32[4,2,128,128]{3,2,1,0:T(8,128)S(1)}, s32[]{:T(128)}) %tuple.215), condition=%wide.while_cond.12, body=%wide.while_body.12.sunk | while | flops 2 | bytes 262261 | solution.py:96
  85.1 34.3 %while.54 = (s32[]{:T(128)}, f32[3,384,384]{2,1,0:T(8,128)S(1)}, s32[4]{0:T(128)}, s32[4]{0:T(128)}, f32[4,3,128,128]{3,2,1,0:T(8,128)S(1)}, /*index=5*/s32[]{:T(128)}, s32[]{:T(128)}, s32[]{:T(128)}) while((s32[]{:T(128)}, f32[3,384,384]{2,1,0:T(8,128)S(1)}, s32[4]{0:T(128)}, s32[4]{0:T(128)}, f32[4,3,128,128]{3,2,1,0:T(8,128)S(1)}, ...), condition=%wide.region_5.6_spmd, body=%wide.region_4.5_spmd.sunk | while | flops 49160 | bytes 983233 | solution.py:109
  119.4 5.4 collective-permute-start.4
  126.2 8.4 %collective-permute-done.4 = f32[3,64,384]{2,1,0:T(8,128)S(1)} collective-permute-done((f32[3,64,384]{2,1,0:T(8,128)S(1)}, f32[3,64,384]{2,1,0:T(8,128)S(1)}, u32[]{:S(2)}, u32[]{:S(2)}) %collective-permute-start.4) | collective-permute-done | bytes 294944 | tf_op jit(solution)/shard_map/ppermute | solution.py:21
  146.4 5.2 scatter-add.44
  168.8 5.1 collective-permute-start.10
  179.3 8.0 %collective-permute-done.11 = f32[2,384,64]{2,1,0:T(8,128)} collective-permute-done((f32[2,384,64]{2,1,0:T(8,128)S(1)}, f32[2,384,64]{2,1,0:T(8,128)}, u32[]{:S(2)}, u32[]{:S(2)}) %collective-permute-start.11) | collective-permute-done | bytes 196640 | tf_op jit(solution)/shard_map/ppermute | solution.py:32
  189.0 8.6 %while.58 = (s32[]{:T(128)}, f32[2,384,384]{2,1,0:T(8,128)S(1)}, s32[4,3]{1,0:T(4,128)S(1)}, f32[4,2,128,128]{3,2,1,0:T(8,128)S(1)}, s32[]{:T(128)}) while((s32[]{:T(128)}, f32[2,384,384]{2,1,0:T(8,128)S(1)}, s32[4,3]{1,0:T(4,128)S(1)}, f32[4,2,128,128]{3,2,1,0:T(8,128)S(1)}, s32[]{:T(128)}) %tuple.221), condition=%wide.while_cond.13, body=%wide.while_body.13.sunk | while | flops 2 | bytes 262261 | solution.py:96
  234.0 31.4 %while.55 = (s32[]{:T(128)}, f32[3,384,384]{2,1,0:T(8,128)S(1)}, s32[4]{0:T(128)S(1)}, s32[4]{0:T(128)S(1)}, f32[4,3,128,128]{3,2,1,0:T(8,128)}, /*index=5*/s32[]{:T(128)}, s32[]{:T(128)}, s32[]{:T(128)}) while((s32[]{:T(128)}, f32[3,384,384]{2,1,0:T(8,128)S(1)}, s32[4]{0:T(128)S(1)}, s32[4]{0:T(128)S(1)}, f32[4,3,128,128]{3,2,1,0:T(8,128)}, ...), condition=%wide.region_10.11_spmd, body=%wide.region_9.10_spmd.sunk | while | flops 49160 | bytes 983233 | solution.py:109
  270.5 11.6 %collective-permute-done.13 = f32[3,64,384]{2,1,0:T(8,128)S(1)} collective-permute-done((f32[3,64,384]{2,1,0:T(8,128)S(1)}, f32[3,64,384]{2,1,0:T(8,128)S(1)}, u32[]{:S(2)}, u32[]{:S(2)}) %collective-permute-start.13) | collective-permute-done | bytes 294944 | tf_op jit(solution)/shard_map/ppermute | solution.py:21
  289.1 5.2 scatter-add.50
  300.4 5.6 collective-permute-start.16
  307.9 5.5 collective-permute-done.17
  313.7 6.4 collective-permute-start.18
  324.8 8.4 %collective-permute-done.19 = f32[2,384,64]{2,1,0:T(8,128)} collective-permute-done((f32[2,384,64]{2,1,0:T(8,128)S(1)}, f32[2,384,64]{2,1,0:T(8,128)}, u32[]{:S(2)}, u32[]{:S(2)}) %collective-permute-start.19) | collective-permute-done | bytes 196640 | tf_op jit(solution)/shard_map/ppermute | solution.py:32
  334.8 8.8 %while.59 = (s32[]{:T(128)}, f32[2,384,384]{2,1,0:T(8,128)S(1)}, s32[4,3]{1,0:T(4,128)S(1)}, f32[4,2,128,128]{3,2,1,0:T(8,128)S(1)}, s32[]{:T(128)}) while((s32[]{:T(128)}, f32[2,384,384]{2,1,0:T(8,128)S(1)}, s32[4,3]{1,0:T(4,128)S(1)}, f32[4,2,128,128]{3,2,1,0:T(8,128)S(1)}, s32[]{:T(128)}) %tuple.227), condition=%wide.while_cond.14, body=%wide.while_body.14.sunk | while | flops 2 | bytes 262261 | solution.py:96
  378.4 33.5 %while.56 = (s32[]{:T(128)}, f32[3,384,384]{2,1,0:T(8,128)S(1)}, s32[4]{0:T(128)S(1)}, s32[4]{0:T(128)S(1)}, f32[4,3,128,128]{3,2,1,0:T(8,128)}, /*index=5*/s32[]{:T(128)}, s32[]{:T(128)}, s32[]{:T(128)}) while((s32[]{:T(128)}, f32[3,384,384]{2,1,0:T(8,128)S(1)}, s32[4]{0:T(128)S(1)}, s32[4]{0:T(128)S(1)}, f32[4,3,128,128]{3,2,1,0:T(8,128)}, ...), condition=%wide.region_15.16_spmd, body=%wide.region_14.15_spmd.sunk | while | flops 49160 | bytes 983233 | solution.py:109
  412.8 5.4 collective-permute-start.20
  424.7 6.0 collective-permute-done.21
  439.3 237.8 %all-reduce.2.cloned.1.call-done = f32[147456]{0:T(1024)} async-done(((f32[147456]{0:T(1024)}), f32[147456]{0:T(1024)}) %all-reduce.2.cloned.1.call-update) | async-done | bytes 589840 | tf_op jit(solution)/shard_map/psum | solution.py:39
  681.1 5.2 scatter-add.56
  (288 shorter events, 286.3 us)
Async XLA Ops:
  7.2 669.9 %all-reduce.2.cloned.1.call-start = ((), (), s32[]{:S(2)}) async-start(), calls=%async_computation | async-start | bytes 1179648 | tf_op jit(solution)/shard_map/psum | solution.py:39
  8.3 9.0 %collective-permute-start = (f32[2,64,256]{2,1,0:T(8,128)S(1)}, f32[2,64,256]{2,1,0:T(8,128)S(1)}, u32[]{:S(2)}, u32[]{:S(2)}) collective-permute-start(f32[2,64,256]{2,1,0:T(8,128)S(1)} %get-tuple-element.572), channel_id=1, source_target_pairs={{0,16},{16,32},{32,48},{48,64},{64,80},{80,96},{96,112},{112,128},... | collective-permute-start | bytes 393224 | tf_op jit(solution)/shard_map/ppermute | solution.py:31
  14.0 12.4 %collective-permute-start.1 = (f32[2,64,256]{2,1,0:T(8,128)S(1)}, f32[2,64,256]{2,1,0:T(8,128)S(1)}, u32[]{:S(2)}, u32[]{:S(2)}) collective-permute-start(f32[2,64,256]{2,1,0:T(8,128)S(1)} %get-tuple-element.571), channel_id=1, source_target_pairs={{16,0},{32,16},{48,32},{64,48},{80,64},{96,80},{112,96},{128,112},... | collective-permute-start | bytes 393224 | tf_op jit(solution)/shard_map/ppermute | solution.py:32
  26.6 6.6 collective-permute-start.2
  28.6 12.7 %collective-permute-start.3 = (f32[2,384,64]{2,1,0:T(8,128)S(1)}, f32[2,384,64]{2,1,0:T(8,128)S(1)}, u32[]{:S(2)}, u32[]{:S(2)}) collective-permute-start(f32[2,384,64]{2,1,0:T(8,128)S(1)} %get-tuple-element.562), channel_id=1, source_target_pairs={{1,0},{2,1},{3,2},{4,3},{5,4},{6,5},{7,6},{8,7},{9,8},{10,9},{11,1... | collective-permute-start | bytes 589832 | tf_op jit(solution)/shard_map/ppermute | solution.py:32
  119.4 15.2 %collective-permute-start.4 = (f32[3,64,384]{2,1,0:T(8,128)S(1)}, f32[3,64,384]{2,1,0:T(8,128)S(1)}, u32[]{:S(2)}, u32[]{:S(2)}) collective-permute-start(f32[3,64,384]{2,1,0:T(8,128)S(1)} %get-tuple-element.550), channel_id=1, source_target_pairs={{0,16},{16,32},{32,48},{48,64},{64,80},{80,96},{96,112},{112,128},... | collective-permute-start | bytes 884744 | tf_op jit(solution)/shard_map/ppermute | solution.py:21
  124.9 14.5 %collective-permute-start.5 = (f32[3,64,384]{2,1,0:T(8,128)S(1)}, f32[3,64,384]{2,1,0:T(8,128)S(1)}, u32[]{:S(2)}, u32[]{:S(2)}) collective-permute-start(f32[3,64,384]{2,1,0:T(8,128)S(1)} %get-tuple-element.549), channel_id=1, source_target_pairs={{16,0},{32,16},{48,32},{64,48},{80,64},{96,80},{112,96},{128,112},... | collective-permute-start | bytes 884744 | tf_op jit(solution)/shard_map/ppermute | solution.py:21
  139.6 6.6 collective-permute-start.6
  141.8 11.9 %collective-permute-start.7 = (f32[3,256,64]{2,1,0:T(8,128)S(1)}, f32[3,256,64]{2,1,0:T(8,128)S(1)}, u32[]{:S(2)}, u32[]{:S(2)}) collective-permute-start(f32[3,256,64]{2,1,0:T(8,128)S(1)} %get-tuple-element.555), channel_id=1, source_target_pairs={{1,0},{2,1},{3,2},{4,3},{5,4},{6,5},{7,6},{8,7},{9,8},{10,9},{11,1... | collective-permute-start | bytes 589832 | tf_op jit(solution)/shard_map/ppermute | solution.py:21
  158.2 5.6 collective-permute-start.8
  161.9 6.6 collective-permute-start.9
  168.8 9.8 %collective-permute-start.10 = (f32[2,384,64]{2,1,0:T(8,128)S(1)}, f32[2,384,64]{2,1,0:T(8,128)S(1)}, u32[]{:S(2)}, u32[]{:S(2)}) collective-permute-start(f32[2,384,64]{2,1,0:T(8,128)S(1)} %get-tuple-element.559), channel_id=1, source_target_pairs={{0,1},{1,2},{2,3},{3,4},{4,5},{5,6},{6,7},{7,8},{8,9},{9,10},{10,1... | collective-permute-start | bytes 589832 | tf_op jit(solution)/shard_map/ppermute | solution.py:31
  173.9 13.5 %collective-permute-start.11 = (f32[2,384,64]{2,1,0:T(8,128)S(1)}, f32[2,384,64]{2,1,0:T(8,128)}, u32[]{:S(2)}, u32[]{:S(2)}) collective-permute-start(f32[2,384,64]{2,1,0:T(8,128)S(1)} %get-tuple-element.560), channel_id=1, source_target_pairs={{1,0},{2,1},{3,2},{4,3},{5,4},{6,5},{7,6},{8,7},{9,8},{10,9},{11,1... | collective-permute-start | bytes 589832 | tf_op jit(solution)/shard_map/ppermute | solution.py:32
  266.7 15.3 %collective-permute-start.13 = (f32[3,64,384]{2,1,0:T(8,128)S(1)}, f32[3,64,384]{2,1,0:T(8,128)S(1)}, u32[]{:S(2)}, u32[]{:S(2)}) collective-permute-start(f32[3,64,384]{2,1,0:T(8,128)S(1)} %get-tuple-element.547), channel_id=1, source_target_pairs={{16,0},{32,16},{48,32},{64,48},{80,64},{96,80},{112,96},{128,112},... | collective-permute-start | bytes 884744 | tf_op jit(solution)/shard_map/ppermute | solution.py:21
  282.3 6.6 collective-permute-start.14
  284.5 11.3 %collective-permute-start.15 = (f32[3,256,64]{2,1,0:T(8,128)S(1)}, f32[3,256,64]{2,1,0:T(8,128)S(1)}, u32[]{:S(2)}, u32[]{:S(2)}) collective-permute-start(f32[3,256,64]{2,1,0:T(8,128)S(1)} %get-tuple-element.553), channel_id=1, source_target_pairs={{1,0},{2,1},{3,2},{4,3},{5,4},{6,5},{7,6},{8,7},{9,8},{10,9},{11,1... | collective-permute-start | bytes 589832 | tf_op jit(solution)/shard_map/ppermute | solution.py:21
  300.4 7.5 %collective-permute-start.16 = (f32[2,64,256]{2,1,0:T(8,128)S(1)}, f32[2,64,256]{2,1,0:T(8,128)S(1)}, u32[]{:S(2)}, u32[]{:S(2)}) collective-permute-start(f32[2,64,256]{2,1,0:T(8,128)S(1)} %get-tuple-element.565), channel_id=1, source_target_pairs={{0,16},{16,32},{32,48},{48,64},{64,80},{80,96},{96,112},{112,128},... | collective-permute-start | bytes 393224 | tf_op jit(solution)/shard_map/ppermute | solution.py:31
  306.0 7.4 %collective-permute-start.17 = (f32[2,64,256]{2,1,0:T(8,128)S(1)}, f32[2,64,256]{2,1,0:T(8,128)S(1)}, u32[]{:S(2)}, u32[]{:S(2)}) collective-permute-start(f32[2,64,256]{2,1,0:T(8,128)S(1)} %get-tuple-element.566), channel_id=1, source_target_pairs={{16,0},{32,16},{48,32},{64,48},{80,64},{96,80},{112,96},{128,112},... | collective-permute-start | bytes 393224 | tf_op jit(solution)/shard_map/ppermute | solution.py:32
  313.7 11.1 %collective-permute-start.18 = (f32[2,384,64]{2,1,0:T(8,128)S(1)}, f32[2,384,64]{2,1,0:T(8,128)S(1)}, u32[]{:S(2)}, u32[]{:S(2)}) collective-permute-start(f32[2,384,64]{2,1,0:T(8,128)S(1)} %get-tuple-element.557), channel_id=1, source_target_pairs={{0,1},{1,2},{2,3},{3,4},{4,5},{5,6},{6,7},{7,8},{8,9},{9,10},{10,1... | collective-permute-start | bytes 589832 | tf_op jit(solution)/shard_map/ppermute | solution.py:31
  320.1 13.1 %collective-permute-start.19 = (f32[2,384,64]{2,1,0:T(8,128)S(1)}, f32[2,384,64]{2,1,0:T(8,128)}, u32[]{:S(2)}, u32[]{:S(2)}) collective-permute-start(f32[2,384,64]{2,1,0:T(8,128)S(1)} %get-tuple-element.558), channel_id=1, source_target_pairs={{1,0},{2,1},{3,2},{4,3},{5,4},{6,5},{7,6},{8,7},{9,8},{10,9},{11,1... | collective-permute-start | bytes 589832 | tf_op jit(solution)/shard_map/ppermute | solution.py:32
  412.8 10.1 %collective-permute-start.20 = (f32[3,64,384]{2,1,0:T(8,128)}, f32[3,64,384]{2,1,0:T(8,128)}, u32[]{:S(2)}, u32[]{:S(2)}) collective-permute-start(f32[3,64,384]{2,1,0:T(8,128)} %get-tuple-element.546), channel_id=1, source_target_pairs={{0,16},{16,32},{32,48},{48,64},{64,80},{80,96},{96,112},{112,128},... | collective-permute-start | bytes 884744 | tf_op jit(solution)/shard_map/ppermute | solution.py:21
  418.2 12.4 %collective-permute-start.21 = (f32[3,64,384]{2,1,0:T(8,128)}, f32[3,64,384]{2,1,0:T(8,128)S(1)}, u32[]{:S(2)}, u32[]{:S(2)}) collective-permute-start(f32[3,64,384]{2,1,0:T(8,128)} %get-tuple-element.545), channel_id=1, source_target_pairs={{16,0},{32,16},{48,32},{64,48},{80,64},{96,80},{112,96},{128,112},... | collective-permute-start | bytes 884744 | tf_op jit(solution)/shard_map/ppermute | solution.py:21
  434.2 245.7 %collective-permute-start.22 = (f32[3,256,64]{2,1,0:T(8,128)S(1)}, f32[3,256,64]{2,1,0:T(8,128)}, u32[]{:S(2)}, u32[]{:S(2)}) collective-permute-start(f32[3,256,64]{2,1,0:T(8,128)S(1)} %get-tuple-element.552), channel_id=1, source_target_pairs={{0,1},{1,2},{2,3},{3,4},{4,5},{5,6},{6,7},{7,8},{8,9},{9,10},{10,1... | collective-permute-start | bytes 589832 | tf_op jit(solution)/shard_map/ppermute | solution.py:21
  436.1 250.2 %collective-permute-start.23 = (f32[3,256,64]{2,1,0:T(8,128)S(1)}, f32[3,256,64]{2,1,0:T(8,128)}, u32[]{:S(2)}, u32[]{:S(2)}) collective-permute-start(f32[3,256,64]{2,1,0:T(8,128)S(1)} %get-tuple-element.551), channel_id=1, source_target_pairs={{1,0},{2,1},{3,2},{4,3},{5,4},{6,5},{7,6},{8,7},{9,8},{10,9},{11,1... | collective-permute-start | bytes 589832 | tf_op jit(solution)/shard_map/ppermute | solution.py:21
  (19 other events, 244.5 us)
Sparse Core Ops, SparseCore 0:
  421.8 255.2 all-reduce.1
where the time goes:
time: 712 us; the launch traced here: 700 us
  waiting for transfers between devices  331 us (46%)
  local copies, waits for them, and re-layouts  109 us (15%)
  matrix products  99.5 us (14%)
  starting transfers between devices  68.4 us (10%)
  loops' own time  45.7 us (6%)
  other arithmetic  29.6 us (4%)
  between operations  15.6 us (2%)
    psum x1, waiting for transfers between devices, together(): subtotal = lax.psum(flat, axis)  238 us
    another operation x3, loops' own time, scatter_patches(): return lax.fori_loop(0, stacked.shape[0], add_patch, buffer)  44.8 us
    ppermute x6, waiting for transfers between devices, padded_2(): after = lax.ppermute(first, axis, down)  43.6 us
    ppermute x12, waiting for transfers between devices, from_behind(): return lax.ppermute(block, axis, route)  41.8 us
    ppermute x12, starting transfers between devices, from_behind(): return lax.ppermute(block, axis, route)  29.8 us
    ppermute x6, starting transfers between devices, padded_2(): before = lax.ppermute(last, axis, up)  28.5 us
    scatter-add x6, local copies, waits for them, and re-layouts, owner_totals(): center.at[:, :, :half_patch].add(from_left).at[:, :, -half_patch:]  28.3 us
    dynamic_update_slice x12, local copies, waits for them, and re-layouts, add_patch(): return lax.dynamic_update_slice(current, region + stacked[position], corner)  26.2 us
  transfers between devices with their start and end apart: 25, of which 22 were waited for; matrix products, arithmetic and copies ran while one was open for 4% of the time, Pallas kernels for 0%

commit v1 on v0

v1 whole, which is shorter than its diff:
```python
import functools
import math

import jax
import jax.numpy as jnp
import ml_dtypes
import numpy as np
from jax import lax
from jax.experimental import pallas as pl
from jax.experimental.pallas import tpu as pltpu
from jax.sharding import PartitionSpec as P

N = 128
MODES = 4
TILE = 256
POS = 4
BATCHES = 3
HALF = 64
PADROWS = 384
FAR = 100000

AMP_FLOOR = 0.25
OBJECT_REG = 0.5
PROBE_REG = 1.0

MESH = pl.DeviceIdType.MESH
VM = pl.BlockSpec(memory_space=pltpu.VMEM)
SM = pl.BlockSpec(memory_space=pltpu.SMEM)


def tables():
    k = np.arange(N)
    ang = (k[:, None] * k[None, :] % N) * (2.0 * math.pi / N)
    fr, fi = np.cos(ang) / math.sqrt(N), -np.sin(ang) / math.sqrt(N)
    a = np.block([[fr, fi], [-fi, fr]])
    b = np.block([[fr, -fi], [fi, fr]])

    def split(m):
        hi = m.astype(np.float32).astype(ml_dtypes.bfloat16)
        lo = (m - hi.astype(np.float64)).astype(np.float32).astype(ml_dtypes.bfloat16)
        return hi, lo

    ah, al = split(a)
    bh, bl = split(b)
    right = lambda h, l: np.concatenate([h, h, l], axis=0)
    left = lambda h, l: np.concatenate([h, h, l], axis=1)
    return right(ah, al), left(bh, bl), left(ah, al), right(bh, bl)


def lanes(shape):
    return lax.broadcasted_iota(jnp.int32, shape, 1)


def split_hi_lo(x):
    hi = x.astype(jnp.bfloat16)
    lo = (x - hi.astype(jnp.float32)).astype(jnp.bfloat16)
    return hi, lo


def dot(a, b):
    return jnp.dot(a, b, preferred_element_type=jnp.float32)


def right_mul(x, table):
    hi, lo = split_hi_lo(x)
    return dot(jnp.concatenate([hi, lo, hi], axis=1), table)


def left_mul(table, x):
    hi, lo = split_hi_lo(x)
    return dot(table, jnp.concatenate([hi, lo, hi], axis=0))


def compute_kernel(batch, offs, info, obj, hl, hr, probe, amp, gin, a3r, b3l, a3l, b3r,
                   center, left, right, linv, gout, pad, buf, light, ltg):
    lane = lanes((N, N))
    for ch in range(2):
        pad[ch, 1] = obj[ch, :, 0:128]
        pad[ch, 2] = obj[ch, :, 128:256]
    pad[0, 0] = pltpu.roll(hl[...], HALF, 1)
    pad[1, 0] = hl[...]
    pad[0, 3] = hr[...]
    pad[1, 3] = pltpu.roll(hr[...], HALF, 1)
    buf[...] = jnp.zeros(buf.shape, jnp.float32)
    light[...] = jnp.zeros(light.shape, jnp.float32)
    gout[...] = gin[...]
    total = jnp.zeros((N, N), jnp.float32)
    for m in range(MODES):
        total += probe[0, m] * probe[0, m] + probe[1, m] * probe[1, m]
    ltg[...] = total

    def place(ref, rows, c0, value):
        t = lax.shift_right_logical(c0, 7)
        s = lax.bitwise_and(c0, 127)
        turned = pltpu.roll(value, s, 1)
        ref[t, rows] += jnp.where(lane >= s, turned, 0.0)
        ref[t + 1, rows] += jnp.where(lane < s, turned, 0.0)

    def light_step(i, carry):
        block = i // POS
        p = i % POS
        cr = block // 3
        rr = block % 3
        r = offs[cr, rr, 0, batch * 8 + p * 2] + (rr - 1) * TILE
        c = offs[cr, rr, 0, batch * 8 + p * 2 + 1] + (cr - 1) * TILE

        @pl.when((r > -192) & (r < 320) & (c > -128) & (c < 256))
        def _():
            place(light, pl.ds(r + 192, N), c + 128, ltg[...])

        return carry

    lax.fori_loop(0, 9 * POS, light_step, 0)

    def step(p, carry):
        r0 = offs[1, 1, 0, batch * 8 + p * 2] + HALF
        c0 = offs[1, 1, 0, batch * 8 + p * 2 + 1] + 128
        t = lax.shift_right_logical(c0, 7)
        s = lax.bitwise_and(c0, 127)
        rows = pl.ds(r0, N)
        back = lax.bitwise_and(128 - s, 127)

        def cut(ch):
            one = pltpu.roll(pad[ch, t, rows], back, 1)
            two = pltpu.roll(pad[ch, t + 1, rows], back, 1)
            return jnp.where(lane < 128 - s, one, two)

        pr, pi = cut(0), cut(1)
        waves = []
        for m in range(MODES):
            qr, qi = probe[0, m], probe[1, m]
            waves.append(jnp.concatenate([qr * pr - qi * pi, qr * pi + qi * pr], axis=1))
        half = right_mul(jnp.concatenate(waves, axis=0), a3r[...])
        rows_of = [half[m * N:(m + 1) * N] for m in range(MODES)]
        stacked = jnp.concatenate(
            [jnp.concatenate([h[:, :N] for h in rows_of], axis=1),
             jnp.concatenate([h[:, N:] for h in rows_of], axis=1)], axis=0)
        far = left_mul(b3l[...], stacked)
        inten = jnp.zeros((N, N), jnp.float32)
        for m in range(MODES):
            fr, fi = far[:N, m * N:(m + 1) * N], far[N:, m * N:(m + 1) * N]
            inten += fr * fr + fi * fi
        factor = amp[p] * lax.rsqrt(jnp.maximum(inten, AMP_FLOOR * AMP_FLOOR)) - 1.0
        factor = jnp.concatenate([factor] * MODES, axis=1)
        factor = jnp.concatenate([factor] * 2, axis=0)
        back_half = left_mul(a3l[...], far * factor)
        lhs = jnp.concatenate(
            [jnp.concatenate([back_half[:N, m * N:(m + 1) * N], back_half[N:, m * N:(m + 1) * N]], axis=1)
             for m in range(MODES)], axis=0)
        change = right_mul(lhs, b3r[...])
        tr = jnp.zeros((N, N), jnp.float32)
        ti = jnp.zeros((N, N), jnp.float32)
        for m in range(MODES):
            qr, qi = probe[0, m], probe[1, m]
            cr, ci = change[m * N:(m + 1) * N, :N], change[m * N:(m + 1) * N, N:]
            tr += qr * cr + qi * ci
            ti += qr * ci - qi * cr
            gout[m] += pr * cr + pi * ci
            gout[MODES + m] += pr * ci - pi * cr
        gout[2 * MODES] += pr * pr + pi * pi
        place(buf.at[0], rows, c0, tr)
        place(buf.at[1], rows, c0, ti)
        return carry

    lax.fori_loop(0, POS, step, 0)

    for ch in range(2):
        center[ch, :, 0:128] = buf[ch, 1]
        center[ch, :, 128:256] = buf[ch, 2]
    wide = lanes((PADROWS, N))
    left[...] = jnp.where(wide < HALF, pltpu.roll(buf[0, 0], HALF, 1), buf[1, 0])
    right[...] = jnp.where(wide < HALF, buf[0, 3], pltpu.roll(buf[1, 3], HALF, 1))
    row = lax.broadcasted_iota(jnp.int32, (PADROWS, N), 0)
    low = jnp.where(info[0] == 0, HALF, 0)
    high = jnp.where(info[0] == info[1] - 1, HALF + TILE, PADROWS)
    inside = (row >= low) & (row < high)
    for t in range(2):
        linv[:, t * 128:t * 128 + 128] = jnp.where(inside, 1.0 / (light[t + 1, 128:512] + OBJECT_REG), 0.0)


def run_compute(batch, offs, info, obj, hl, hr, probe, amp, gin, tabs):
    f = jnp.float32
    return pl.pallas_call(
        functools.partial(compute_kernel, batch),
        out_shape=(
            jax.ShapeDtypeStruct((2, PADROWS, TILE), f),
            jax.ShapeDtypeStruct((PADROWS, N), f),
            jax.ShapeDtypeStruct((PADROWS, N), f),
            jax.ShapeDtypeStruct((PADROWS, TILE), f),
            jax.ShapeDtypeStruct((2 * MODES + 1, N, N), f),
        ),
        in_specs=[SM, SM] + [VM] * 10,
        out_specs=(VM,) * 5,
        scratch_shapes=[
            pltpu.VMEM((2, 4, PADROWS, N), f),
            pltpu.VMEM((2, 4, PADROWS, N), f),
            pltpu.VMEM((4, 640, N), f),
            pltpu.VMEM((N, N), f),
        ],
        compiler_params=pltpu.CompilerParams(vmem_limit_bytes=28 * 2**20),
        name="compute",
    )(offs, info, obj, hl, hr, probe, amp, gin, *tabs)


def position():
    row, col = lax.axis_index("row"), lax.axis_index("col")
    rows, cols = lax.axis_size("row"), lax.axis_size("col")
    up = (row > 0, {"row": jnp.maximum(row - 1, 0), "col": col})
    down = (row < rows - 1, {"row": jnp.minimum(row + 1, rows - 1), "col": col})
    left = (col > 0, {"row": row, "col": jnp.maximum(col - 1, 0)})
    right = (col < cols - 1, {"row": row, "col": jnp.minimum(col + 1, cols - 1)})
    return up, down, left, right


def greet(sides):
    barrier = pltpu.get_barrier_semaphore()
    for there, device in sides:
        @pl.when(there)
        def _(device=device):
            pl.semaphore_signal(barrier, inc=1, device_id=device, device_id_type=MESH)
    pl.semaphore_wait(barrier, sum(there.astype(jnp.int32) for there, _ in sides))


class Link:
    def __init__(self, src, dst, send, recv, to, source):
        self.there, device = to
        self.source = source[0]
        self.copy = pltpu.make_async_remote_copy(
            src_ref=src, dst_ref=dst, send_sem=send, recv_sem=recv,
            device_id=device, device_id_type=MESH)

    def start(self):
        @pl.when(self.there)
        def _():
            self.copy.start()

    def arrived(self):
        @pl.when(self.source)
        def _():
            self.copy.wait_recv()

    def sent(self):
        @pl.when(self.there)
        def _():
            self.copy.wait_send()


def strips(re0, im0, re1, im1):
    lane = lanes(re0.shape)
    left = jnp.where(lane < HALF, re0, pltpu.roll(im0, HALF, 1))
    right = jnp.where(lane < HALF, pltpu.roll(re1, HALF, 1), im1)
    return left, right


def first_kernel(obj, offs, out, hl_out, hr_out, offs_out,
                 from_up, from_down, sl, sr, hl, hr, table, send, recv):
    up, down, left, right = position()
    for ref in (from_up, from_down, hl, hr):
        ref[...] = jnp.zeros(ref.shape, ref.dtype)
    table[...] = jnp.full(table.shape, FAR, jnp.int32)
    table[1, 1] = offs[...]
    greet((up, down, left, right))

    count = iter(range(100))

    def link(src, dst, to, source):
        i = next(count)
        return Link(src, dst, send.at[i], recv.at[i], to, source)

    rows = [
        link(obj.at[:, pl.ds(0, HALF), :], from_down, up, down),
        link(obj.at[:, pl.ds(TILE - HALF, HALF), :], from_up, down, up),
        link(table.at[1, 1], table.at[1, 2], up, down),
        link(table.at[1, 1], table.at[1, 0], down, up),
    ]
    for c in rows:
        c.start()

    def cols(at, size):
        a = link(sl.at[pl.ds(at, size)], hr.at[pl.ds(at, size)], left, right)
        b = link(sr.at[pl.ds(at, size)], hl.at[pl.ds(at, size)], right, left)
        return [a, b]

    every = list(rows)
    a, b = strips(obj[0, :, 0:128], obj[1, :, 0:128], obj[0, :, 128:256], obj[1, :, 128:256])
    sl[HALF:HALF + TILE] = a
    sr[HALF:HALF + TILE] = b
    mid = cols(HALF, TILE)
    for c in mid:
        c.start()
    every += mid
    out[:, HALF:HALF + TILE, :] = obj[...]
    for c in rows:
        c.arrived()
    more = [
        link(table.at[1], table.at[2], left, right),
        link(table.at[1], table.at[0], right, left),
    ]
    for c in more:
        c.start()
    for ref, at in ((from_up, 0), (from_down, HALF + TILE)):
        a, b = strips(ref[0, :, 0:128], ref[1, :, 0:128], ref[0, :, 128:256], ref[1, :, 128:256])
        sl[at:at + HALF] = a
        sr[at:at + HALF] = b
        both = cols(at, HALF)
        for c in both:
            c.start()
        more += both
        out[:, at:at + HALF, :] = ref[...]
    every += more
    for c in mid + more:
        c.arrived()
    hl_out[...] = hl[...]
    hr_out[...] = hr[...]
    offs_out[...] = table[...]
    for c in every:
        c.sent()


def run_first(obj, offs):
    f = jnp.float32
    return pl.pallas_call(
        first_kernel,
        out_shape=(
            jax.ShapeDtypeStruct((2, PADROWS, TILE), f),
            jax.ShapeDtypeStruct((PADROWS, N), f),
            jax.ShapeDtypeStruct((PADROWS, N), f),
            jax.ShapeDtypeStruct((3, 3, 8, N), jnp.int32),
        ),
        in_specs=[VM, VM],
        out_specs=(VM,) * 4,
        scratch_shapes=[
            pltpu.VMEM((2, HALF, TILE), f),
            pltpu.VMEM((2, HALF, TILE), f),
            pltpu.VMEM((PADROWS, N), f),
            pltpu.VMEM((PADROWS, N), f),
            pltpu.VMEM((PADROWS, N), f),
            pltpu.VMEM((PADROWS, N), f),
            pltpu.VMEM((3, 3, 8, N), jnp.int32),
            pltpu.SemaphoreType.DMA((12,)),
            pltpu.SemaphoreType.DMA((12,)),
        ],
        compiler_params=pltpu.CompilerParams(collective_id=0, has_side_effects=True, vmem_limit_bytes=14 * 2**20),
        name="first",
    )(obj, offs)


def fold_kernel(last, center, ls, rs, obj, linv, out, *rest):
    if last:
        from_left, from_right, total, from_up, from_down, send, recv = rest
        reach = HALF
    else:
        hl_out, hr_out, from_left, from_right, total, from_up, from_down, sl, sr, hl, hr, send, recv = rest
        reach = N
    up, down, left, right = position()
    for ref in (from_left, from_right, from_up, from_down) + (() if last else (hl, hr)):
        ref[...] = jnp.zeros(ref.shape, ref.dtype)
    greet((up, down, left, right))
    count = iter(range(100))

    def link(src, dst, to, source):
        i = next(count)
        return Link(src, dst, send.at[i], recv.at[i], to, source)

    every = []
    cols = {}
    for at in (0, 256, 128):
        w = pl.ds(at, N)
        cols[at] = [link(ls.at[w], from_right.at[w], left, right),
                    link(rs.at[w], from_left.at[w], right, left)]
        for c in cols[at]:
            c.start()
        every += cols[at]

    def add_cols(at):
        for c in cols[at]:
            c.arrived()
        w = slice(at, at + N)
        lane = lanes((N, N))
        a, b = from_left[w], from_right[w]
        total[0, w, 0:128] = center[0, w, 0:128] + jnp.where(lane < HALF, a, 0.0)
        total[1, w, 0:128] = center[1, w, 0:128] + jnp.where(lane < HALF, pltpu.roll(a, HALF, 1), 0.0)
        total[0, w, 128:256] = center[0, w, 128:256] + jnp.where(lane >= HALF, pltpu.roll(b, HALF, 1), 0.0)
        total[1, w, 128:256] = center[1, w, 128:256] + jnp.where(lane >= HALF, b, 0.0)

    add_cols(0)
    to_up = link(total.at[:, pl.ds(0, reach), :], from_down, up, down)
    to_up.start()
    add_cols(256)
    to_down = link(total.at[:, pl.ds(PADROWS - reach, reach), :], from_up, down, up)
    to_down.start()
    add_cols(128)
    every += [to_up, to_down]

    halos = []

    def update(at, size, extra):
        w = slice(at, at + size)
        lv = linv[w]
        new = []
        for ch in range(2):
            t = total[ch, w]
            if extra is not None:
                t = t + extra[ch]
            new.append(obj[ch, w] + t * lv)
            if last:
                out[ch, at - HALF:at - HALF + size] = new[ch]
            else:
                out[ch, w] = new[ch]
        if not last:
            a, b = strips(new[0][:, 0:128], new[1][:, 0:128], new[0][:, 128:256], new[1][:, 128:256])
            sl[w] = a
            sr[w] = b
            d = pl.ds(at, size)
            both = [link(sl.at[d], hr.at[d], left, right), link(sr.at[d], hl.at[d], right, left)]
            for c in both:
                c.start()
            halos.extend(both)

    update(N, N, None)
    start = HALF if last else 0
    to_down.arrived()
    update(start, reach, from_up)
    to_up.arrived()
    update(256, reach, from_down)
    every += halos
    if not last:
        for c in halos:
            c.arrived()
        hl_out[...] = hl[...]
        hr_out[...] = hr[...]
    for c in every:
        c.sent()


def run_fold(last, ident, center, ls, rs, obj, linv):
    f = jnp.float32
    reach = HALF if last else N
    strip = pltpu.VMEM((PADROWS, N), f)
    strip_out = jax.ShapeDtypeStruct((PADROWS, N), f)
    if last:
        shapes = (jax.ShapeDtypeStruct((2, TILE, TILE), f),)
    else:
        shapes = (jax.ShapeDtypeStruct((2, PADROWS, TILE), f), strip_out, strip_out)
    return pl.pallas_call(
        functools.partial(fold_kernel, last),
        out_shape=shapes,
        in_specs=[VM] * 5,
        out_specs=(VM,) * len(shapes),
        scratch_shapes=[
            strip, strip,
            pltpu.VMEM((2, PADROWS, TILE), f),
            pltpu.VMEM((2, reach, TILE), f),
            pltpu.VMEM((2, reach, TILE), f),
        ] + ([] if last else [strip] * 4) + [
            pltpu.SemaphoreType.DMA((14,)),
            pltpu.SemaphoreType.DMA((14,)),
        ],
        compiler_params=pltpu.CompilerParams(collective_id=ident, has_side_effects=True, vmem_limit_bytes=14 * 2**20),
        name="fold_last" if last else f"fold{ident}",
    )(center, ls, rs, obj, linv)


TILES = 144
HALFT = 72
PIECE = 9
SUB = 3


def reduce_kernel(g, out, r1, s1, r2, s2, r3, z, fin, ag1, ag2, ag3, send, recv):
    row, col = lax.axis_index("row"), lax.axis_index("col")
    x, zh = row // 4, row % 4
    core, group = col % 2, col // 2
    partner = {"row": row, "col": col + 1 - 2 * core}

    def in_group(d):
        return lax.rem(group + d, 8)

    def group_dev(k):
        return {"row": row, "col": k * 2 + core}

    def x_dev(k):
        return {"row": k * 4 + zh, "col": col}

    def z_dev(k):
        return {"row": x * 4 + k, "col": col}

    peers = [partner] + [group_dev(in_group(d)) for d in range(1, 8)]
    peers += [x_dev(lax.rem(x + d, 4)) for d in range(1, 4)]
    peers += [z_dev(lax.rem(zh + d, 4)) for d in range(1, 4)]

    s2[pl.ds(PIECE, 12 - PIECE)] = jnp.zeros((12 - PIECE, 8, N), jnp.float32)
    barrier = pltpu.get_barrier_semaphore()
    for device in peers:
        pl.semaphore_signal(barrier, inc=1, device_id=device, device_id_type=MESH)
    pl.semaphore_wait(barrier, len(peers))

    count = iter(range(100))
    every = []

    def go(src, dst, device):
        i = next(count)
        c = pltpu.make_async_remote_copy(
            src_ref=src, dst_ref=dst, send_sem=send.at[i], recv_sem=recv.at[i],
            device_id=device, device_id_type=MESH)
        c.start()
        every.append(c)
        return c

    c = go(g.at[pl.ds((1 - core) * HALFT, HALFT)], r1, partner)
    c.wait_recv()
    s1[...] = g[pl.ds(core * HALFT, HALFT)] + r1[...]

    cs = [go(s1.at[pl.ds(in_group(d) * PIECE, PIECE)], r2.at[d - 1], group_dev(in_group(d))) for d in range(1, 8)]
    acc = s1[pl.ds(group * PIECE, PIECE)]
    for d, c in enumerate(cs):
        c.wait_recv()
        acc = acc + r2[d]
    s2[pl.ds(0, PIECE)] = acc

    cs = [go(s2.at[pl.ds(lax.rem(x + d, 4) * SUB, SUB)], r3.at[d - 1], x_dev(lax.rem(x + d, 4))) for d in range(1, 4)]
    acc = s2[pl.ds(x * SUB, SUB)]
    for d, c in enumerate(cs):
        c.wait_recv()
        acc = acc + r3[d]
    z[0] = acc

    cs = [go(z.at[0], z.at[d], z_dev(lax.rem(zh + d, 4))) for d in range(1, 4)]
    for c in cs:
        c.wait_recv()
    acc = z[lax.rem(zh, 4)]
    for k in range(1, 4):
        acc = acc + z[lax.rem(zh - k + 4, 4)]
    fin[...] = acc

    cs = [go(fin, ag1.at[pl.ds(x * SUB, SUB)], x_dev(lax.rem(x + d, 4))) for d in range(1, 4)]
    ag1[pl.ds(x * SUB, SUB)] = fin[...]
    for c in cs:
        c.wait_recv()

    cs = [go(ag1.at[pl.ds(0, PIECE)], ag2.at[pl.ds(group * PIECE, PIECE)], group_dev(in_group(d))) for d in range(1, 8)]
    ag2[pl.ds(group * PIECE, PIECE)] = ag1[pl.ds(0, PIECE)]
    for c in cs:
        c.wait_recv()

    c = go(ag2, ag3.at[pl.ds(core * HALFT, HALFT)], partner)
    ag3[pl.ds(core * HALFT, HALFT)] = ag2[...]
    c.wait_recv()

    inv = lax.rsqrt(ag3[pl.ds(128, 16)] + PROBE_REG)
    for k in range(8):
        out[pl.ds(16 * k, 16)] = ag3[pl.ds(16 * k, 16)] * inv
    for c in every:
        c.wait_send()


def run_reduce(g):
    f = jnp.float32
    shape = lambda *n: pltpu.VMEM(n + (8, N), f)
    return pl.pallas_call(
        reduce_kernel,
        out_shape=jax.ShapeDtypeStruct((128, 8, N), f),
        in_specs=[VM],
        out_specs=VM,
        scratch_shapes=[
            shape(HALFT), shape(HALFT), shape(7, PIECE), shape(12), shape(3, SUB),
            shape(4, SUB), shape(SUB), shape(12), shape(HALFT), shape(TILES),
            pltpu.SemaphoreType.DMA((25,)),
            pltpu.SemaphoreType.DMA((25,)),
        ],
        compiler_params=pltpu.CompilerParams(collective_id=9, has_side_effects=True, vmem_limit_bytes=14 * 2**20),
        name="reduce",
    )(g)


def on_device(object_field, probe, amplitudes, offsets):
    info = jnp.stack([lax.axis_index("row"), jnp.int32(lax.axis_size("row"))]).astype(jnp.int32)
    mine = jnp.pad(offsets.reshape(1, 24), ((0, 7), (0, N - 24)))
    tabs = [jnp.asarray(t) for t in tables()]
    obj, hl, hr, offs = run_first(object_field, mine)
    grads = jnp.zeros((2 * MODES + 1, N, N), jnp.float32)
    amps = amplitudes.reshape(BATCHES, POS, N, N)
    for b in range(BATCHES):
        center, ls, rs, linv, grads = run_compute(b, offs, info, obj, hl, hr, probe, amps[b], grads, tabs)
        if b < BATCHES - 1:
            obj, hl, hr = run_fold(False, b + 1, center, ls, rs, obj, linv)
        else:
            (obj,) = run_fold(True, b + 1, center, ls, rs, obj, linv)
    step = run_reduce(grads.reshape(TILES, 8, N))
    return obj, step.reshape(2, MODES, N, N)


def solution(mesh):
    placed = (
        P(None, "row", "col"),
        P(),
        P("row", "col", None, None, None, None),
        P("row", "col", None, None, None),
    )
    return jax.shard_map(
        on_device,
        mesh=mesh,
        in_specs=placed,
        out_specs=(P(None, "row", "col"), P()),
        check_vma=False,
    )
```

time: 712 us -> 160 us (0.22); the launches traced: 700 us -> 160 us
  waiting for transfers between devices: 331 us -> 0 us
  Pallas kernels: 0 us -> 154 us
  local copies, waits for them, and re-layouts: 109 us -> 4.61 us
  matrix products: 99.5 us -> 0 us
  starting transfers between devices: 68.4 us -> 0 us
  loops' own time: 45.7 us -> 0 us
  other arithmetic: 29.6 us -> 0.08 us
  between operations: 15.6 us -> 0.81 us
    psum x1 -> x0, waiting for transfers between devices: 238 us -> none  [together(): subtotal = lax.psum(flat, axis)]
    pallas_call x0 -> x8, Pallas kernels: none -> 154 us  [the longest x3 61.7 us: run_fold(): pl.pallas_call(functools.partial(fold_kernel, last), out_shape=shapes, in...]
    dot_general x48 -> x0, matrix products: 99.5 us -> none  [the longest x6 14.9 us: transform(): jnp.einsum('...jk,kl->...jl', left_real, signed, precision=PRECISE_DOT)]
    ppermute x24 -> x0, waiting for transfers between devices: 93.6 us -> none  [the longest x6 43.6 us: padded_2(): after = lax.ppermute(first, axis, down)]
    ppermute x24 -> x0, starting transfers between devices: 68.4 us -> none  [the longest x12 29.8 us: from_behind(): return lax.ppermute(block, axis, route)]
    another operation x6 -> x0, loops' own time: 45.7 us -> none  [the longest x3 44.8 us: scatter_patches(): return lax.fori_loop(0, stacked.shape[0], add_patch, buffer)]
    scatter-add x6 -> x0, local copies, waits for them, and re-layouts: 28.3 us -> none  [owner_totals(): center.at[:, :, :half_patch].add(from_left).at[:, :, -half_patch:]]
    dynamic_update_slice x12 -> x0, local copies, waits for them, and re-layouts: 26.2 us -> none  [add_patch(): return lax.dynamic_update_slice(current, region + stacked[position], corner)]
  transfers between devices with their start and end apart: 25 -> 0, of which waited for: 22 -> 0; matrix products, arithmetic and copies ran while one was open for 4% -> 0% of each run, Pallas kernels for 0% -> 0%
where the time goes in v1:
time: 160 us
  Pallas kernels  154 us (96%)
  local copies, waits for them, and re-layouts  4.61 us (3%)
    pallas_call x3, Pallas kernels, run_fold(): pl.pallas_call(functools.partial(fold_kernel, last), out_shape=shapes, in...  61.7 us
    pallas_call x1, Pallas kernels, run_reduce(): pl.pallas_call(reduce_kernel, out_shape=jax.ShapeDtypeStruct((128, 8, N),...  38.5 us
    pallas_call x3, Pallas kernels, run_compute(): pl.pallas_call(functools.partial(compute_kernel, batch), out_shape=(jax.S...  35 us
    pallas_call x1, Pallas kernels, run_first(): pl.pallas_call(first_kernel, out_shape=(jax.ShapeDtypeStruct((2, PADROWS,...  18.9 us
    unnamed x17, local copies, waits for them, and re-layouts  3.23 us

profile of v1, /device:TPU:1, one launch (start us, length us, event | category | flops | bytes accessed | tf_op | source)
XLA Modules:
  0.0 159.6 jit_solution(12069342289244512050)
XLA Ops:
  0.6 0.1 pad_add_fusion.info
  0.7 0.6 copy-done.6
  1.3 0.1 copy.11
  1.4 0.1 reshape.20
  1.5 0.0 copy-start.2
  1.5 0.0 copy-start.3
  1.6 0.0 copy-start.4
  1.6 1.3 slice_bitcast_fusion
  2.8 0.0 copy-done.5
  2.8 0.0 copy-start
  2.8 18.9 %first.1 = (f32[2,384,256]{2,1,0:T(8,128)S(1)}, f32[384,128]{1,0:T(8,128)S(1)}, f32[384,128]{1,0:T(8,128)S(1)}, s32[3,3,8,128]{3,2,1,0:T(8,128)S(1)}) custom-call(f32[2,256,256]{2,1,0:T(8,128)S(1)} %copy-done.5, s32[8,128]{1,0:T(8,128)S(1)} %pad.4.offs), custom_call_target="tpu_custom_call" | custom-call | tf_op jit(solution)/shard_map/first/pallas_call | solution.py:322
  21.8 0.0 copy-start.1
  21.8 0.0 copy-done.2
  21.8 0.0 copy-done.3
  21.9 0.9 copy-done.1
  22.8 11.8 %compute.3 = (f32[2,384,256]{2,1,0:T(8,128)S(1)}, f32[384,128]{1,0:T(8,128)S(1)}, f32[384,128]{1,0:T(8,128)S(1)}, f32[384,256]{1,0:T(8,128)S(1)}, f32[9,128,128]{2,1,0:T(8,128)S(1)}) custom-call(s32[3,3,8,128]{3,2,1,0:T(8,128)S(1)} %get-tuple-element.27.offs, s32[2]{0:T(128)S(1)} %pad_add_fusion.info, f32[2,384,256]{2,1,0:T(8,128)S(1)} %get-tuple-element.28.obj, ...), custom_call_target="tpu_custom_call" | custom-call | tf_op jit(solution)/shard_map/compute/pallas_call | solution.py:183
  34.5 23.5 %fold1.1 = (f32[2,384,256]{2,1,0:T(8,128)S(1)}, f32[384,128]{1,0:T(8,128)S(1)}, f32[384,128]{1,0:T(8,128)S(1)}) custom-call(f32[2,384,256]{2,1,0:T(8,128)S(1)} %get-tuple-element.31.center, f32[384,128]{1,0:T(8,128)S(1)} %get-tuple-element.32.ls, f32[384,128]{1,0:T(8,128)S(1)} %get-tuple-element.33.rs, f32[2,384,256]{2,1,0:T(8,128)S(1)} %get-tuple-element.28.obj, ...), custom_call_target="tpu_custom_call" | custom-call | tf_op jit(solution)/shard_map/fold1/pallas_call | solution.py:445
  58.1 11.7 %compute.4 = (f32[2,384,256]{2,1,0:T(8,128)S(1)}, f32[384,128]{1,0:T(8,128)S(1)}, f32[384,128]{1,0:T(8,128)S(1)}, f32[384,256]{1,0:T(8,128)S(1)}, f32[9,128,128]{2,1,0:T(8,128)S(1)}) custom-call(s32[3,3,8,128]{3,2,1,0:T(8,128)S(1)} %get-tuple-element.27.offs, s32[2]{0:T(128)S(1)} %pad_add_fusion.info, f32[2,384,256]{2,1,0:T(8,128)S(1)} %get-tuple-element.35.obj, ...), custom_call_target="tpu_custom_call" | custom-call | tf_op jit(solution)/shard_map/compute/pallas_call | solution.py:183
  69.8 28.4 %fold2.1 = (f32[2,384,256]{2,1,0:T(8,128)S(1)}, f32[384,128]{1,0:T(8,128)S(1)}, f32[384,128]{1,0:T(8,128)S(1)}) custom-call(f32[2,384,256]{2,1,0:T(8,128)S(1)} %get-tuple-element.39.center, f32[384,128]{1,0:T(8,128)S(1)} %get-tuple-element.40.ls, f32[384,128]{1,0:T(8,128)S(1)} %get-tuple-element.41.rs, f32[2,384,256]{2,1,0:T(8,128)S(1)} %get-tuple-element.35.obj, ...), custom_call_target="tpu_custom_call" | custom-call | tf_op jit(solution)/shard_map/fold2/pallas_call | solution.py:445
  98.2 11.5 %compute.5 = (f32[2,384,256]{2,1,0:T(8,128)S(1)}, f32[384,128]{1,0:T(8,128)S(1)}, f32[384,128]{1,0:T(8,128)S(1)}, f32[384,256]{1,0:T(8,128)S(1)}, f32[9,128,128]{2,1,0:T(8,128)S(1)}) custom-call(s32[3,3,8,128]{3,2,1,0:T(8,128)S(1)} %get-tuple-element.27.offs, s32[2]{0:T(128)S(1)} %pad_add_fusion.info, f32[2,384,256]{2,1,0:T(8,128)S(1)} %get-tuple-element.43.obj, ...), custom_call_target="tpu_custom_call" | custom-call | tf_op jit(solution)/shard_map/compute/pallas_call | solution.py:183
  109.7 9.8 %fold_last.1 = f32[2,256,256]{2,1,0:T(8,128)S(1)} custom-call(f32[2,384,256]{2,1,0:T(8,128)S(1)} %get-tuple-element.47.center, f32[384,128]{1,0:T(8,128)S(1)} %get-tuple-element.48.ls, f32[384,128]{1,0:T(8,128)S(1)} %get-tuple-element.49.rs, f32[2,384,256]{2,1,0:T(8,128)S(1)} %get-tuple-element.43.obj, f32[384,256]{1,0:T(8,128)S(1)} %get-tuple-element.50.linv), custom_call_target="tpu_custom_call" | custom-call | tf_op jit(solution)/shard_map/fold_last/pallas_call | solution.py:445
  119.5 38.5 %reduce.1 = f32[128,8,128]{2,1,0:T(8,128)S(1)} custom-call(f32[144,8,128]{2,1,0:T(8,128)S(1)} %bitcast.10), custom_call_target="tpu_custom_call" | custom-call | tf_op jit(solution)/shard_map/reduce/pallas_call | solution.py:560
  158.0 0.8 copy.14
  158.8 0.8 copy.15
  (6 shorter events, 0.1 us)
Async XLA Ops:
  0.6 0.7 copy-start.6
  1.3 1.5 copy-start.5
  1.5 20.3 %copy-start.2 = (bf16[256,768]{1,0:T(8,128)(2,1)S(1)}, bf16[256,768]{1,0:T(8,128)(2,1)}, u32[]{:S(2)}) copy-start(bf16[256,768]{1,0:T(8,128)(2,1)} %constant.21.clone.a3l) | copy-start | bytes 1179652
  1.5 20.3 %copy-start.3 = (bf16[256,768]{1,0:T(8,128)(2,1)S(1)}, bf16[256,768]{1,0:T(8,128)(2,1)}, u32[]{:S(2)}) copy-start(bf16[256,768]{1,0:T(8,128)(2,1)} %constant.20.clone.b3l) | copy-start | bytes 1179652
  1.6 20.3 %copy-start.4 = (bf16[768,256]{1,0:T(8,128)(2,1)S(1)}, bf16[768,256]{1,0:T(8,128)(2,1)}, u32[]{:S(2)}) copy-start(bf16[768,256]{1,0:T(8,128)(2,1)} %constant.19.clone.a3r) | copy-start | bytes 1179652
  2.8 19.0 %copy-start = (f32[2,4,128,128]{3,2,1,0:T(8,128)S(1)}, f32[2,4,128,128]{3,2,1,0:T(8,128)}, u32[]{:S(2)}) copy-start(f32[2,4,128,128]{3,2,1,0:T(8,128)} %probe.5) | copy-start | bytes 1572868
  21.8 1.0 copy-start.1

commit v2 on v0

v2 whole, which is shorter than its diff:
```python
import functools
import math

import jax
import jax.numpy as jnp
import ml_dtypes
import numpy as np
from jax import lax
from jax.experimental import pallas as pl
from jax.experimental.pallas import tpu as pltpu
from jax.sharding import PartitionSpec as P

N = 128
MODES = 4
TILE = 256
POS = 4
BATCHES = 3
HALF = 64
PADROWS = 384
FAR = 100000

AMP_FLOOR = 0.25
OBJECT_REG = 0.5
PROBE_REG = 1.0

MESH = pl.DeviceIdType.MESH
VM = pl.BlockSpec(memory_space=pltpu.VMEM)
SM = pl.BlockSpec(memory_space=pltpu.SMEM)


def tables():
    k = np.arange(N)
    ang = (k[:, None] * k[None, :] % N) * (2.0 * math.pi / N)
    fr, fi = np.cos(ang) / math.sqrt(N), -np.sin(ang) / math.sqrt(N)
    a = np.block([[fr, fi], [-fi, fr]])
    b = np.block([[fr, -fi], [fi, fr]])

    def split(m):
        hi = m.astype(np.float32).astype(ml_dtypes.bfloat16)
        lo = (m - hi.astype(np.float64)).astype(np.float32).astype(ml_dtypes.bfloat16)
        return hi, lo

    ah, al = split(a)
    bh, bl = split(b)
    right = lambda h, l: np.concatenate([h, h, l], axis=0)
    left = lambda h, l: np.concatenate([h, h, l], axis=1)
    return right(ah, al), left(bh, bl), left(ah, al), right(bh, bl)


def lanes(shape):
    return lax.broadcasted_iota(jnp.int32, shape, 1)


def split_hi_lo(x):
    hi = x.astype(jnp.bfloat16)
    lo = (x - hi.astype(jnp.float32)).astype(jnp.bfloat16)
    return hi, lo


def dot(a, b):
    return jnp.dot(a, b, preferred_element_type=jnp.float32)


def right_mul(x, table):
    hi, lo = split_hi_lo(x)
    return dot(jnp.concatenate([hi, lo, hi], axis=1), table)


def left_mul(table, x):
    hi, lo = split_hi_lo(x)
    return dot(table, jnp.concatenate([hi, lo, hi], axis=0))


def position():
    row, col = lax.axis_index("row"), lax.axis_index("col")
    rows, cols = lax.axis_size("row"), lax.axis_size("col")
    up = (row > 0, {"row": jnp.maximum(row - 1, 0), "col": col})
    down = (row < rows - 1, {"row": jnp.minimum(row + 1, rows - 1), "col": col})
    left = (col > 0, {"row": row, "col": jnp.maximum(col - 1, 0)})
    right = (col < cols - 1, {"row": row, "col": jnp.minimum(col + 1, cols - 1)})
    return up, down, left, right


def greet(sides, others=()):
    barrier = pltpu.get_barrier_semaphore()
    for there, device in sides:
        @pl.when(there)
        def _(device=device):
            pl.semaphore_signal(barrier, inc=1, device_id=device, device_id_type=MESH)
    for device in others:
        pl.semaphore_signal(barrier, inc=1, device_id=device, device_id_type=MESH)


def greeted(sides, others=()):
    barrier = pltpu.get_barrier_semaphore()
    pl.semaphore_wait(barrier, sum(there.astype(jnp.int32) for there, _ in sides) + len(others))


class Link:
    def __init__(self, src, dst, send, recv, to, source):
        self.there, device = to
        self.source = source[0]
        self.copy = pltpu.make_async_remote_copy(
            src_ref=src, dst_ref=dst, send_sem=send, recv_sem=recv,
            device_id=device, device_id_type=MESH)

    def start(self):
        @pl.when(self.there)
        def _():
            self.copy.start()

    def arrived(self):
        @pl.when(self.source)
        def _():
            self.copy.wait_recv()

    def sent(self):
        @pl.when(self.there)
        def _():
            self.copy.wait_send()


def clear_missing(pairs):
    for there, ref in pairs:
        @pl.when(jnp.logical_not(there))
        def _(ref=ref):
            ref[...] = jnp.zeros(ref.shape, ref.dtype)


def turn(x):
    return pltpu.roll(x, HALF, 1)


def halo_strips(re, im):
    lane = lanes(re.shape)
    ti = turn(im)
    return jnp.where(lane < HALF, ti, re), jnp.where(lane < HALF, re, ti)


def first_kernel(obj, offs, out, offs_out, me, sl, sr, hl, hr, table, send, recv):
    up, down, left, right = position()
    lane = lanes((TILE, N))
    table[...] = jnp.full(table.shape, FAR, jnp.int32)
    table[1, 1] = offs[...]
    clear_missing([(left[0], hl), (right[0], hr),
                   (up[0], me.at[:, :, pl.ds(0, HALF), :]),
                   (down[0], me.at[:, :, pl.ds(PADROWS - HALF, HALF), :])])
    greet((up, down, left, right))
    own = slice(HALF, HALF + TILE)
    for ch in range(2):
        a, b = turn(obj[ch, :, 0:128]), turn(obj[ch, :, 128:256])
        me[1, ch, own] = jnp.where(lane < HALF, b, a)
        me[0, ch, own] = jnp.where(lane < HALF, a, b)
    greeted((up, down, left, right))

    count = iter(range(100))

    def link(src, dst, to, source):
        i = next(count)
        return Link(src, dst, send.at[i], recv.at[i], to, source)

    def rows(which):
        top, bottom = pl.ds(HALF, HALF), pl.ds(TILE, HALF)
        above, below = pl.ds(0, HALF), pl.ds(PADROWS - HALF, HALF)
        return [link(me.at[which, :, top, :], me.at[which, :, below, :], up, down),
                link(me.at[which, :, bottom, :], me.at[which, :, above, :], down, up)]

    def cols(at, size):
        w = slice(at, at + size)
        a, b = halo_strips(me[1, 0, w], me[1, 1, w])
        sl[w] = a
        sr[w] = b
        d = pl.ds(at, size)
        both = [link(sl.at[d], hr.at[d], left, right), link(sr.at[d], hl.at[d], right, left)]
        for c in both:
            c.start()
        return both

    tell = [link(table.at[1, 1], table.at[1, 2], up, down),
            link(table.at[1, 1], table.at[1, 0], down, up)]
    edge = rows(1)
    middle = rows(0)
    for c in tell + edge:
        c.start()
    late = cols(HALF, TILE)
    for c in middle:
        c.start()
    for c in tell:
        c.arrived()
    more = [link(table.at[1], table.at[2], left, right),
            link(table.at[1], table.at[0], right, left)]
    for c in more:
        c.start()
    late += more
    edge[1].arrived()
    late += cols(0, HALF)
    edge[0].arrived()
    late += cols(PADROWS - HALF, HALF)
    for c in middle:
        c.arrived()
    for ch in range(2):
        out[ch, 1] = me[0, ch]
    for c in late:
        c.arrived()
    finish_tiles(out, me, hl, hr)
    offs_out[...] = table[...]
    for c in tell + edge + middle + late:
        c.sent()


def finish_tiles(out, me, hl, hr):
    wide = lanes((PADROWS, N))
    out[0, 0] = jnp.where(wide < HALF, hl[...], me[1, 0])
    out[1, 0] = jnp.where(wide < HALF, turn(hl[...]), me[1, 1])
    out[0, 2] = jnp.where(wide < HALF, me[1, 0], hr[...])
    out[1, 2] = jnp.where(wide < HALF, me[1, 1], turn(hr[...]))


def run_first(obj, offs):
    f = jnp.float32
    strip = pltpu.VMEM((PADROWS, N), f)
    return pl.pallas_call(
        first_kernel,
        out_shape=(
            jax.ShapeDtypeStruct((2, 3, PADROWS, N), f),
            jax.ShapeDtypeStruct((3, 3, 8, N), jnp.int32),
        ),
        in_specs=[VM, VM],
        out_specs=(VM,) * 2,
        scratch_shapes=[
            pltpu.VMEM((2, 2, PADROWS, N), f),
            strip, strip, strip, strip,
            pltpu.VMEM((3, 3, 8, N), jnp.int32),
            pltpu.SemaphoreType.DMA((14,)),
            pltpu.SemaphoreType.DMA((14,)),
        ],
        compiler_params=pltpu.CompilerParams(collective_id=0, has_side_effects=True, vmem_limit_bytes=14 * 2**20),
        name="first",
    )(obj, offs)


def spread(dest, value, s):
    lane = lanes((N, N))
    turned = pltpu.roll(value, s, 1)
    dest[0, N:2 * N] = jnp.where(lane >= s, turned, 0.0)
    dest[1, N:2 * N] = jnp.where(lane < s, turned, 0.0)


def window(src, r0, t, i, k):
    j = k - t
    hit = (j == 0) | (j == 1)
    start = jnp.where(hit, jnp.clip(N + N * i - r0, 0, 2 * N), 0)
    return src[jnp.where(hit, j, 0), pl.ds(start, N)]


def transforms(batch, offs, tiles, probe, amp, gout, z, a3r, b3l, a3l, b3r):
    lane = lanes((N, N))

    def step(p, carry):
        r0 = offs[1, 1, 0, batch * 8 + p * 2] + HALF
        c0 = offs[1, 1, 0, batch * 8 + p * 2 + 1] + HALF
        t = lax.shift_right_arithmetic(c0, 7)
        s = lax.bitwise_and(c0, 127)
        rows = pl.ds(r0, N)
        back = lax.bitwise_and(128 - s, 127)
        after = jnp.minimum(t + 1, 2)

        def cut(ch):
            one = pltpu.roll(tiles[ch, t, rows], back, 1)
            two = pltpu.roll(tiles[ch, after, rows], back, 1)
            return jnp.where(lane < 128 - s, one, two)

        pr, pi = cut(0), cut(1)
        waves = []
        for m in range(MODES):
            qr, qi = probe[0, m], probe[1, m]
            waves.append(jnp.concatenate([qr * pr - qi * pi, qr * pi + qi * pr], axis=1))
        half = right_mul(jnp.concatenate(waves, axis=0), a3r[...])
        rows_of = [half[m * N:(m + 1) * N] for m in range(MODES)]
        stacked = jnp.concatenate(
            [jnp.concatenate([h[:, :N] for h in rows_of], axis=1),
             jnp.concatenate([h[:, N:] for h in rows_of], axis=1)], axis=0)
        far = left_mul(b3l[...], stacked)
        inten = jnp.zeros((N, N), jnp.float32)
        for m in range(MODES):
            fr, fi = far[:N, m * N:(m + 1) * N], far[N:, m * N:(m + 1) * N]
            inten += fr * fr + fi * fi
        factor = amp[batch, p] * lax.rsqrt(jnp.maximum(inten, AMP_FLOOR * AMP_FLOOR)) - 1.0
        factor = jnp.concatenate([factor] * MODES, axis=1)
        factor = jnp.concatenate([factor] * 2, axis=0)
        back_half = left_mul(a3l[...], far * factor)
        lhs = jnp.concatenate(
            [jnp.concatenate([back_half[:N, m * N:(m + 1) * N], back_half[N:, m * N:(m + 1) * N]], axis=1)
             for m in range(MODES)], axis=0)
        change = right_mul(lhs, b3r[...])
        tr = jnp.zeros((N, N), jnp.float32)
        ti = jnp.zeros((N, N), jnp.float32)
        for m in range(MODES):
            qr, qi = probe[0, m], probe[1, m]
            cr, ci = change[m * N:(m + 1) * N, :N], change[m * N:(m + 1) * N, N:]
            tr += qr * cr + qi * ci
            ti += qr * ci - qi * cr
            gout[m] += pr * cr + pi * ci
            gout[MODES + m] += pr * ci - pi * cr
        gout[2 * MODES] += pr * pr + pi * pi
        spread(z.at[p, 0], tr, s)
        spread(z.at[p, 1], ti, s)
        return carry

    lax.fori_loop(0, POS, step, 0)


def light_maps(batch, offs, probe, zl, light):
    lane = lanes((N, N))
    total = jnp.zeros((N, N), jnp.float32)
    for m in range(MODES):
        total += probe[0, m] * probe[0, m] + probe[1, m] * probe[1, m]
    for j in range(2):
        zl[j, 0:N] = jnp.zeros((N, N), jnp.float32)
        zl[j, 2 * N:] = jnp.zeros((N, N), jnp.float32)
    zl[2, 0:N] = total
    light[...] = jnp.zeros(light.shape, jnp.float32)

    def step(i, carry):
        block, p = i // POS, i % POS
        cr, rr = block // 3, block % 3
        r0 = offs[cr, rr, 0, batch * 8 + p * 2] + (rr - 1) * TILE + HALF
        c0 = offs[cr, rr, 0, batch * 8 + p * 2 + 1] + (cr - 1) * TILE + HALF
        t = lax.shift_right_arithmetic(c0, 7)
        spread(zl, zl[2, 0:N], lax.bitwise_and(c0, 127))
        for b in range(3):
            w = slice(b * N, b * N + N)
            light[0, w] += window(zl, r0, t, b, 1)
            light[1, w] += jnp.where(lane < HALF, window(zl, r0, t, b, 2), window(zl, r0, t, b, 0))
        return carry

    lax.fori_loop(0, 9 * POS, step, 0)
    row, rows = lax.axis_index("row"), lax.axis_size("row")
    place = lax.broadcasted_iota(jnp.int32, (PADROWS, N), 0)
    low = jnp.where(row == 0, HALF, 0)
    high = jnp.where(row == rows - 1, HALF + TILE, PADROWS)
    inside = (place >= low) & (place < high)
    for j in range(2):
        light[j] = jnp.where(inside, 1.0 / (light[j] + OBJECT_REG), 0.0)


TILES = 144
HALFT = 72
PIECE = 9
SUB = 3


class Reduction:
    def __init__(self, g, out, r1, s1, r2, s2, r3, z, fin, ag1, ag2, ag3, send, recv):
        self.refs = (g, out, r1, s1, r2, s2, r3, z, fin, ag1, ag2, ag3)
        self.send, self.recv = send, recv
        self.count = iter(range(100))
        self.every = []
        row, col = lax.axis_index("row"), lax.axis_index("col")
        self.x, self.zh = row // 4, row % 4
        self.core, self.group = col % 2, col // 2
        self.row, self.col = row, col
        self.partner = {"row": row, "col": col + 1 - 2 * self.core}
        self.peers = [self.partner]
        self.peers += [self.group_dev(self.in_group(d)) for d in range(1, 8)]
        self.peers += [self.x_dev(d) for d in range(1, 4)]
        self.peers += [self.z_dev(d) for d in range(1, 4)]

    def in_group(self, d):
        return lax.rem(self.group + d, 8)

    def group_dev(self, k):
        return {"row": self.row, "col": k * 2 + self.core}

    def x_dev(self, d):
        return {"row": lax.rem(self.x + d, 4) * 4 + self.zh, "col": self.col}

    def z_dev(self, d):
        return {"row": self.x * 4 + lax.rem(self.zh + d, 4), "col": self.col}

    def go(self, src, dst, device):
        i = next(self.count)
        c = pltpu.make_async_remote_copy(
            src_ref=src, dst_ref=dst, send_sem=self.send.at[i], recv_sem=self.recv.at[i],
            device_id=device, device_id_type=MESH)
        c.start()
        self.every.append(c)
        return c

    def stages(self):
        g, out, r1, s1, r2, s2, r3, z, fin, ag1, ag2, ag3 = self.refs
        x, zh, core, group, go, in_group = self.x, self.zh, self.core, self.group, self.go, self.in_group
        s2[pl.ds(PIECE, 12 - PIECE)] = jnp.zeros((12 - PIECE, 8, N), jnp.float32)
        c = go(g.at[pl.ds((1 - core) * HALFT, HALFT)], r1, self.partner)
        yield
        c.wait_recv()
        s1[...] = g[pl.ds(core * HALFT, HALFT)] + r1[...]
        cs = [go(s1.at[pl.ds(in_group(d) * PIECE, PIECE)], r2.at[d - 1], self.group_dev(in_group(d))) for d in range(1, 8)]
        yield
        acc = s1[pl.ds(group * PIECE, PIECE)]
        for d, c in enumerate(cs):
            c.wait_recv()
            acc = acc + r2[d]
        s2[pl.ds(0, PIECE)] = acc
        cs = [go(s2.at[pl.ds(lax.rem(x + d, 4) * SUB, SUB)], r3.at[d - 1], self.x_dev(d)) for d in range(1, 4)]
        yield
        acc = s2[pl.ds(x * SUB, SUB)]
        for d, c in enumerate(cs):
            c.wait_recv()
            acc = acc + r3[d]
        z[0] = acc
        cs = [go(z.at[0], z.at[d], self.z_dev(d)) for d in range(1, 4)]
        yield
        for c in cs:
            c.wait_recv()
        acc = z[lax.rem(zh, 4)]
        for k in range(1, 4):
            acc = acc + z[lax.rem(zh - k + 4, 4)]
        fin[...] = acc
        cs = [go(fin, ag1.at[pl.ds(x * SUB, SUB)], self.x_dev(d)) for d in range(1, 4)]
        ag1[pl.ds(x * SUB, SUB)] = fin[...]
        yield
        for c in cs:
            c.wait_recv()
        cs = [go(ag1.at[pl.ds(0, PIECE)], ag2.at[pl.ds(group * PIECE, PIECE)], self.group_dev(in_group(d))) for d in range(1, 8)]
        ag2[pl.ds(group * PIECE, PIECE)] = ag1[pl.ds(0, PIECE)]
        yield
        for c in cs:
            c.wait_recv()
        c = go(ag2, ag3.at[pl.ds(core * HALFT, HALFT)], self.partner)
        ag3[pl.ds(core * HALFT, HALFT)] = ag2[...]
        yield
        c.wait_recv()
        inv = lax.rsqrt(ag3[pl.ds(128, 16)] + PROBE_REG)
        for k in range(8):
            out[pl.ds(16 * k, 16)] = ag3[pl.ds(16 * k, 16)] * inv
        for c in self.every:
            c.wait_send()
        yield


def reduction_scratch():
    f = jnp.float32
    shape = lambda *n: pltpu.VMEM(n + (8, N), f)
    return [shape(HALFT), shape(HALFT), shape(7, PIECE), shape(12), shape(3, SUB),
            shape(4, SUB), shape(SUB), shape(12), shape(HALFT), shape(TILES),
            pltpu.SemaphoreType.DMA((25,)), pltpu.SemaphoreType.DMA((25,))]


def batch_kernel(batch, last, offs, tiles, probe, amp, gin, a3r, b3l, a3l, b3r, *rest):
    if last:
        out, step_out, gout, flat, z, zl, light, ls, rs, ls_in, rs_in, me, fresh, from_up, from_down, send, recv, *more = rest
        reach = HALF
        red = Reduction(flat, step_out, *more)
        others = red.peers
    else:
        out, gout, z, zl, light, ls, rs, ls_in, rs_in, me, fresh, from_up, from_down, sl, sr, hl, hr, send, recv = rest
        reach = N
        others = ()
    up, down, left, right = sides = position()
    clear_missing([(left[0], rs_in), (right[0], ls_in), (up[0], from_up), (down[0], from_down)])
    if not last:
        clear_missing([(left[0], hl), (right[0], hr)])
    greet(sides, others)

    blank = jnp.zeros((N, N), jnp.float32)
    for p in range(POS):
        for ch in range(2):
            for j in range(2):
                z[p, ch, j, 0:N] = blank
                z[p, ch, j, 2 * N:] = blank
    gout[...] = gin[...]
    transforms(batch, offs, tiles, probe, amp, gout, z, a3r, b3l, a3l, b3r)
    if last:
        flat[...] = gout[...].reshape(TILES, 8, N)
    spots = []
    for p in range(POS):
        r0 = offs[1, 1, 0, batch * 8 + p * 2] + HALF
        c0 = offs[1, 1, 0, batch * 8 + p * 2 + 1] + HALF
        spots.append((p, r0, lax.shift_right_arithmetic(c0, 7)))
    greeted(sides, others)

    count = iter(range(100))

    def link(src, dst, to, source):
        i = next(count)
        return Link(src, dst, send.at[i], recv.at[i], to, source)

    def gathered(ch, i, k):
        acc = None
        for p, r0, t in spots:
            w = window(z.at[p, ch], r0, t, i, k)
            acc = w if acc is None else acc + w
        return acc

    lane = lanes((N, N))
    every = []
    cols = {}

    def send_cols(i):
        w = slice(i * N, i * N + N)
        t0 = [gathered(ch, i, 0) for ch in range(2)]
        t2 = [gathered(ch, i, 2) for ch in range(2)]
        ls[w] = jnp.where(lane < HALF, t0[0], turn(t0[1]))
        rs[w] = jnp.where(lane < HALF, turn(t2[0]), t2[1])
        for ch in range(2):
            me[1, ch, w] = jnp.where(lane < HALF, t2[ch], t0[ch])
        d = pl.ds(i * N, N)
        cols[i] = [link(ls.at[d], ls_in.at[d], left, right), link(rs.at[d], rs_in.at[d], right, left)]
        for c in cols[i]:
            c.start()
        every.extend(cols[i])

    def middle(i):
        for ch in range(2):
            me[0, ch, i * N:i * N + N] = gathered(ch, i, 1)

    def fold_cols(i):
        for c in cols[i]:
            c.arrived()
        w = slice(i * N, i * N + N)
        a, b = ls_in[w], rs_in[w]
        me[1, 0, w] += jnp.where(lane < HALF, a, turn(b))
        me[1, 1, w] += jnp.where(lane < HALF, turn(a), b)

    stage = iter(red.stages()) if last else iter([None] * 20)
    next(stage)
    send_cols(0)
    send_cols(2)
    middle(0)
    row_links = {}

    def rows_pair(which, top):
        if last:
            at = 0 if top else PADROWS - HALF
        else:
            at = 0 if top else PADROWS - N
        d = pl.ds(at, reach)
        if top:
            c = link(me.at[which, :, d, :], from_down.at[which], up, down)
        else:
            c = link(me.at[which, :, d, :], from_up.at[which], down, up)
        c.start()
        every.append(c)
        row_links[which, top] = c

    rows_pair(0, True)
    middle(2)
    rows_pair(0, False)
    send_cols(1)
    middle(1)
    if last:
        next(stage)
    light_maps(batch, offs, probe, zl, light)
    fold_cols(0)
    rows_pair(1, True)
    fold_cols(2)
    rows_pair(1, False)
    fold_cols(1)
    if last:
        next(stage)

    halos = []

    def update(which, at, size, extra):
        w = slice(at, at + size)
        lv = light[which, w]
        mine = lanes((size, N))
        for ch in range(2):
            t = me[which, ch, w]
            if extra is not None:
                t = t + extra[which, ch]
            old = tiles[ch, 1, w] if which == 0 else jnp.where(mine < HALF, tiles[ch, 2, w], tiles[ch, 0, w])
            fresh[which, ch, w] = old + t * lv

    def halo(at, size):
        w = slice(at, at + size)
        a, b = halo_strips(fresh[1, 0, w], fresh[1, 1, w])
        sl[w] = a
        sr[w] = b
        d = pl.ds(at, size)
        both = [link(sl.at[d], hr.at[d], left, right), link(sr.at[d], hl.at[d], right, left)]
        for c in both:
            c.start()
        halos.extend(both)

    update(1, N, N, None)
    if not last:
        halo(N, N)
    update(0, N, N, None)
    if last:
        next(stage)
    start = HALF if last else 0
    row_links[1, False].arrived()
    update(1, start, reach, from_up)
    if not last:
        halo(0, N)
    row_links[1, True].arrived()
    update(1, 2 * N, reach, from_down)
    if not last:
        halo(2 * N, N)
    row_links[0, False].arrived()
    update(0, start, reach, from_up)
    row_links[0, True].arrived()
    update(0, 2 * N, reach, from_down)
    every.extend(halos)
    if last:
        wide = lanes((TILE, N))
        w = slice(HALF, HALF + TILE)
        for ch in range(2):
            m, e = fresh[0, ch, w], fresh[1, ch, w]
            out[ch, :, 0:128] = turn(jnp.where(wide < HALF, m, e))
            out[ch, :, 128:256] = turn(jnp.where(wide < HALF, e, m))
        for _ in stage:
            pass
    else:
        for ch in range(2):
            out[ch, 1] = fresh[0, ch]
        for c in halos:
            c.arrived()
        finish_tiles(out, fresh, hl, hr)
    for c in every:
        c.sent()


def run_batch(batch, last, offs, tiles, probe, amp, gin, tabs):
    f = jnp.float32
    strip = pltpu.VMEM((PADROWS, N), f)
    sums = jax.ShapeDtypeStruct((2 * MODES + 1, N, N), f)
    reach = HALF if last else N
    if last:
        shapes = (jax.ShapeDtypeStruct((2, TILE, TILE), f), jax.ShapeDtypeStruct((128, 8, N), f))
        extra = [pltpu.VMEM((2 * MODES + 1, N, N), f), pltpu.VMEM((TILES, 8, N), f)]
    else:
        shapes = (jax.ShapeDtypeStruct((2, 3, PADROWS, N), f), sums)
        extra = []
    return pl.pallas_call(
        functools.partial(batch_kernel, batch, last),
        out_shape=shapes,
        in_specs=[SM] + [VM] * 8,
        out_specs=(VM,) * len(shapes),
        scratch_shapes=extra + [
            pltpu.VMEM((POS, 2, 2, PADROWS, N), f),
            pltpu.VMEM((3, PADROWS, N), f),
            pltpu.VMEM((2, PADROWS, N), f),
            strip, strip, strip, strip,
            pltpu.VMEM((2, 2, PADROWS, N), f),
            pltpu.VMEM((2, 2, PADROWS, N), f),
            pltpu.VMEM((2, 2, reach, N), f),
            pltpu.VMEM((2, 2, reach, N), f),
        ] + ([] if last else [strip] * 4) + [
            pltpu.SemaphoreType.DMA((16,)),
            pltpu.SemaphoreType.DMA((16,)),
        ] + (reduction_scratch() if last else []),
        compiler_params=pltpu.CompilerParams(
            collective_id=1 + batch, has_side_effects=True, vmem_limit_bytes=36 * 2**20),
        name=f"batch{batch}",
    )(offs, tiles, probe, amp, gin, *tabs)


def on_device(object_field, probe, amplitudes, offsets):
    mine = jnp.pad(offsets.reshape(1, 24), ((0, 7), (0, N - 24)))
    tabs = [jnp.asarray(t) for t in tables()]
    tiles, offs = run_first(object_field, mine)
    grads = jnp.zeros((2 * MODES + 1, N, N), jnp.float32)
    amps = amplitudes.reshape(BATCHES, POS, N, N)
    for b in range(BATCHES - 1):
        tiles, grads = run_batch(b, False, offs, tiles, probe, amps, grads, tabs)
    obj, step = run_batch(BATCHES - 1, True, offs, tiles, probe, amps, grads, tabs)
    return obj, step.reshape(2, MODES, N, N)


def solution(mesh):
    placed = (
        P(None, "row", "col"),
        P(),
        P("row", "col", None, None, None, None),
        P("row", "col", None, None, None),
    )
    return jax.shard_map(
        on_device,
        mesh=mesh,
        in_specs=placed,
        out_specs=(P(None, "row", "col"), P()),
        check_vma=False,
    )
```

time: 712 us -> 136 us (0.19); the launches traced: 700 us -> 136 us
  waiting for transfers between devices: 331 us -> 0 us
  Pallas kernels: 0 us -> 126 us
  local copies, waits for them, and re-layouts: 109 us -> 8.65 us
  matrix products: 99.5 us -> 0 us
  starting transfers between devices: 68.4 us -> 0 us
  loops' own time: 45.7 us -> 0 us
  other arithmetic: 29.6 us -> 0 us
  between operations: 15.6 us -> 0.75 us
    psum x1 -> x0, waiting for transfers between devices: 238 us -> none  [together(): subtotal = lax.psum(flat, axis)]
    pallas_call x0 -> x4, Pallas kernels: none -> 126 us  [the longest x3 109 us: run_batch(): pl.pallas_call(functools.partial(batch_kernel, batch, last), out_shape=sh...]
    dot_general x48 -> x0, matrix products: 99.5 us -> none  [the longest x6 14.9 us: transform(): jnp.einsum('...jk,kl->...jl', left_real, signed, precision=PRECISE_DOT)]
    ppermute x24 -> x0, waiting for transfers between devices: 93.6 us -> none  [the longest x6 43.6 us: padded_2(): after = lax.ppermute(first, axis, down)]
    ppermute x24 -> x0, starting transfers between devices: 68.4 us -> none  [the longest x12 29.8 us: from_behind(): return lax.ppermute(block, axis, route)]
    another operation x6 -> x0, loops' own time: 45.7 us -> none  [the longest x3 44.8 us: scatter_patches(): return lax.fori_loop(0, stacked.shape[0], add_patch, buffer)]
    scatter-add x6 -> x0, local copies, waits for them, and re-layouts: 28.3 us -> none  [owner_totals(): center.at[:, :, :half_patch].add(from_left).at[:, :, -half_patch:]]
    dynamic_update_slice x12 -> x0, local copies, waits for them, and re-layouts: 26.2 us -> none  [add_patch(): return lax.dynamic_update_slice(current, region + stacked[position], corner)]
  transfers between devices with their start and end apart: 25 -> 0, of which waited for: 22 -> 0; matrix products, arithmetic and copies ran while one was open for 4% -> 0% of each run, Pallas kernels for 0% -> 0%
where the time goes in v2:
time: 136 us
  Pallas kernels  126 us (93%)
  local copies, waits for them, and re-layouts  8.65 us (6%)
    pallas_call x3, Pallas kernels, run_batch(): pl.pallas_call(functools.partial(batch_kernel, batch, last), out_shape=sh...  109 us
    pallas_call x1, Pallas kernels, run_first(): pl.pallas_call(first_kernel, out_shape=(jax.ShapeDtypeStruct((2, 3, PADRO...  17.1 us
    unnamed x25, local copies, waits for them, and re-layouts  8.52 us

profile of v2, /device:TPU:1, one launch (start us, length us, event | category | flops | bytes accessed | tf_op | source)
XLA Modules:
  0.0 135.6 jit_solution(17507347110210382418)
XLA Ops:
  0.6 0.0 copy-start
  0.6 0.9 copy.11
  1.5 0.1 reshape.13
  1.6 0.0 copy-start.10
  1.6 1.0 copy-done.10
  2.6 17.1 %first.1 = (f32[2,3,384,128]{3,2,1,0:T(8,128)S(1)}, s32[3,3,8,128]{3,2,1,0:T(8,128)S(1)}) custom-call(f32[2,256,256]{2,1,0:T(8,128)S(1)} %copy-done.10, s32[8,128]{1,0:T(8,128)S(1)} %pad.4.offs), custom_call_target="tpu_custom_call" | custom-call | tf_op jit(solution)/shard_map/first/pallas_call | solution.py:222
  19.8 0.0 copy-done
  19.8 0.0 copy-start.1
  19.8 1.0 copy-done.1
  20.9 0.0 copy-start.3
  20.9 1.0 copy-done.3
  21.9 0.0 copy-start.5
  21.9 1.0 copy-done.5
  22.9 1.0 copy-done.7
  23.9 1.0 copy-done.9
  24.9 31.7 %batch0.1 = (f32[2,3,384,128]{3,2,1,0:T(8,128)S(1)}, f32[9,128,128]{2,1,0:T(8,128)S(1)}) custom-call(s32[3,3,8,128]{3,2,1,0:T(8,128)S(1)} %get-tuple-element.10.offs, f32[2,3,384,128]{3,2,1,0:T(8,128)S(1)} %get-tuple-element.11.tiles, f32[2,4,128,128]{3,2,1,0:T(8,128)S(1)} %copy-done.1, f32[3,4,128,128]{3,2,1,0:T(8,128)S(1)} %bitcast.2, ...), custom_call_target="tpu_custom_call" | custom-call | tf_op jit(solution)/shard_map/batch0/pallas_call | solution.py:637
  56.5 0.0 copy-done.2
  56.5 0.0 copy-done.4
  56.6 0.0 copy-done.6
  56.6 0.0 copy-done.8
  56.6 26.5 %batch1.1 = (f32[2,3,384,128]{3,2,1,0:T(8,128)S(1)}, f32[9,128,128]{2,1,0:T(8,128)S(1)}) custom-call(s32[3,3,8,128]{3,2,1,0:T(8,128)S(1)} %get-tuple-element.10.offs, f32[2,3,384,128]{3,2,1,0:T(8,128)S(1)} %get-tuple-element.12.tiles, f32[2,4,128,128]{3,2,1,0:T(8,128)S(1)} %copy-done.2, f32[3,4,128,128]{3,2,1,0:T(8,128)S(1)} %bitcast.3, ...), custom_call_target="tpu_custom_call" | custom-call | tf_op jit(solution)/shard_map/batch1/pallas_call | solution.py:637
  83.0 51.0 %batch2.1 = (f32[2,256,256]{2,1,0:T(8,128)S(1)}, f32[128,8,128]{2,1,0:T(8,128)S(1)}) custom-call(s32[3,3,8,128]{3,2,1,0:T(8,128)S(1)} %get-tuple-element.10.offs, f32[2,3,384,128]{3,2,1,0:T(8,128)S(1)} %get-tuple-element.14.tiles, f32[2,4,128,128]{3,2,1,0:T(8,128)S(1)} %copy-done.2, f32[3,4,128,128]{3,2,1,0:T(8,128)S(1)} %bitcast.4, ...), custom_call_target="tpu_custom_call" | custom-call | tf_op jit(solution)/shard_map/batch2/pallas_call | solution.py:637
  134.0 0.8 copy.14
  134.8 0.8 copy.15
  (8 shorter events, 0.1 us)
Async XLA Ops:
  0.6 19.2 %copy-start = (f32[1,1,3,4,128,128]{5,4,3,2,1,0:T(8,128)S(1)}, f32[1,1,3,4,128,128]{5,4,3,2,1,0:T(8,128)}, u32[]{:S(2)}) copy-start(f32[1,1,3,4,128,128]{5,4,3,2,1,0:T(8,128)} %param.10) | copy-start | bytes 2359300
  1.6 1.0 copy-start.10
  19.8 1.0 copy-start.1
  20.9 1.0 copy-start.3
  21.9 1.0 copy-start.5
  22.9 1.0 copy-start.7
  23.9 1.0 copy-start.9
  24.9 31.7 %copy-start.2 = (f32[2,4,128,128]{3,2,1,0:T(8,128)S(1)}, f32[2,4,128,128]{3,2,1,0:T(8,128)}, u32[]{:S(2)}) copy-start(f32[2,4,128,128]{3,2,1,0:T(8,128)} %probe.5) | copy-start | bytes 1572868
  24.9 31.7 %copy-start.4 = (bf16[768,256]{1,0:T(8,128)(2,1)S(1)}, bf16[768,256]{1,0:T(8,128)(2,1)}, u32[]{:S(2)}) copy-start(bf16[768,256]{1,0:T(8,128)(2,1)} %constant.15.clone.b3r) | copy-start | bytes 1179652
  24.9 31.7 %copy-start.6 = (bf16[256,768]{1,0:T(8,128)(2,1)S(1)}, bf16[256,768]{1,0:T(8,128)(2,1)}, u32[]{:S(2)}) copy-start(bf16[256,768]{1,0:T(8,128)(2,1)} %constant.14.clone.a3l) | copy-start | bytes 1179652
  24.9 31.7 %copy-start.8 = (bf16[256,768]{1,0:T(8,128)(2,1)S(1)}, bf16[256,768]{1,0:T(8,128)(2,1)}, u32[]{:S(2)}) copy-start(bf16[256,768]{1,0:T(8,128)(2,1)} %constant.13.clone.b3l) | copy-start | bytes 1179652

commit v3 on v2

--- a/solution.py
+++ b/solution.py
@@ -42,9 +42,7 @@
 
     ah, al = split(a)
     bh, bl = split(b)
-    right = lambda h, l: np.concatenate([h, h, l], axis=0)
-    left = lambda h, l: np.concatenate([h, h, l], axis=1)
-    return right(ah, al), left(bh, bl), left(ah, al), right(bh, bl)
+    return ah, al, bh, bl
 
 
 def lanes(shape):
@@ -61,14 +59,14 @@
     return jnp.dot(a, b, preferred_element_type=jnp.float32)
 
 
-def right_mul(x, table):
+def right_mul(x, th, tl):
     hi, lo = split_hi_lo(x)
-    return dot(jnp.concatenate([hi, lo, hi], axis=1), table)
-
-
-def left_mul(table, x):
+    return dot(jnp.concatenate([hi, lo, hi], axis=1), jnp.concatenate([th, th, tl], axis=0))
+
+
+def left_mul(th, tl, x):
     hi, lo = split_hi_lo(x)
-    return dot(table, jnp.concatenate([hi, lo, hi], axis=0))
+    return dot(jnp.concatenate([th, th, tl], axis=1), jnp.concatenate([hi, lo, hi], axis=0))
 
 
 def position():
@@ -137,8 +135,16 @@
     return jnp.where(lane < HALF, ti, re), jnp.where(lane < HALF, re, ti)
 
 
-def first_kernel(obj, offs, out, offs_out, me, sl, sr, hl, hr, table, send, recv):
+def first_kernel(obj_hbm, offs, *rest):
+    far_refs, rest = rest[:6], rest[6:]
+    out, offs_out, *near_refs = rest[:8]
+    obj, me, sl, sr, hl, hr, table, send, recv, local = rest[8:]
     up, down, left, right = position()
+    load = pltpu.make_async_copy(obj_hbm, obj, local.at[0])
+    load.start()
+    loads = [pltpu.make_async_copy(a, b, local.at[i + 1]) for i, (a, b) in enumerate(zip(far_refs, near_refs))]
+    for c in loads:
+        c.start()
     lane = lanes((TILE, N))
     table[...] = jnp.full(table.shape, FAR, jnp.int32)
     table[1, 1] = offs[...]
@@ -147,6 +153,7 @@
                    (down[0], me.at[:, :, pl.ds(PADROWS - HALF, HALF), :])])
     greet((up, down, left, right))
     own = slice(HALF, HALF + TILE)
+    load.wait()
     for ch in range(2):
         a, b = turn(obj[ch, :, 0:128]), turn(obj[ch, :, 128:256])
         me[1, ch, own] = jnp.where(lane < HALF, b, a)
@@ -204,6 +211,8 @@
         c.arrived()
     finish_tiles(out, me, hl, hr)
     offs_out[...] = table[...]
+    for c in loads:
+        c.wait()
     for c in tell + edge + middle + late:
         c.sent()
 
@@ -216,27 +225,30 @@
     out[1, 2] = jnp.where(wide < HALF, me[1, 1], turn(hr[...]))
 
 
-def run_first(obj, offs):
+def run_first(obj, offs, others):
     f = jnp.float32
     strip = pltpu.VMEM((PADROWS, N), f)
+    hbm = pl.BlockSpec(memory_space=pltpu.HBM)
     return pl.pallas_call(
         first_kernel,
         out_shape=(
             jax.ShapeDtypeStruct((2, 3, PADROWS, N), f),
             jax.ShapeDtypeStruct((3, 3, 8, N), jnp.int32),
-        ),
-        in_specs=[VM, VM],
-        out_specs=(VM,) * 2,
+        ) + tuple(jax.ShapeDtypeStruct(a.shape, a.dtype) for a in others),
+        in_specs=[hbm, VM] + [hbm] * 6,
+        out_specs=(VM,) * 8,
         scratch_shapes=[
+            pltpu.VMEM((2, TILE, TILE), f),
             pltpu.VMEM((2, 2, PADROWS, N), f),
             strip, strip, strip, strip,
             pltpu.VMEM((3, 3, 8, N), jnp.int32),
             pltpu.SemaphoreType.DMA((14,)),
             pltpu.SemaphoreType.DMA((14,)),
+            pltpu.SemaphoreType.DMA((7,)),
         ],
         compiler_params=pltpu.CompilerParams(collective_id=0, has_side_effects=True, vmem_limit_bytes=14 * 2**20),
         name="first",
-    )(obj, offs)
+    )(obj, offs, *others)
 
 
 def spread(dest, value, s):
@@ -253,14 +265,71 @@
     return src[jnp.where(hit, j, 0), pl.ds(start, N)]
 
 
-def transforms(batch, offs, tiles, probe, amp, gout, z, a3r, b3l, a3l, b3r):
+STATIC = ((0, 0, 0), (1, 2 * N, 2))
+MOVING = (2, 3)
+
+
+def spot(offs, block, batch, p):
+    cr, rr = block
+    r0 = offs[cr, rr, 0, batch * 8 + p * 2] + (rr - 1) * TILE + HALF
+    c0 = offs[cr, rr, 0, batch * 8 + p * 2 + 1] + (cr - 1) * TILE + HALF
+    return r0, lax.shift_right_arithmetic(c0, 7), lax.bitwise_and(c0, 127)
+
+
+def terms(pr, pi, probe, measured, gout, gin, first, ah, al, bh, bl):
+    waves = []
+    for m in range(MODES):
+        qr, qi = probe[0, m], probe[1, m]
+        waves.append(jnp.concatenate([qr * pr - qi * pi, qr * pi + qi * pr], axis=1))
+    half = right_mul(jnp.concatenate(waves, axis=0), ah[...], al[...])
+    rows_of = [half[m * N:(m + 1) * N] for m in range(MODES)]
+    stacked = jnp.concatenate(
+        [jnp.concatenate([h[:, :N] for h in rows_of], axis=1),
+         jnp.concatenate([h[:, N:] for h in rows_of], axis=1)], axis=0)
+    far = left_mul(bh[...], bl[...], stacked)
+    inten = jnp.zeros((N, N), jnp.float32)
+    for m in range(MODES):
+        fr, fi = far[:N, m * N:(m + 1) * N], far[N:, m * N:(m + 1) * N]
+        inten += fr * fr + fi * fi
+    factor = measured * lax.rsqrt(jnp.maximum(inten, AMP_FLOOR * AMP_FLOOR)) - 1.0
+    factor = jnp.concatenate([factor] * MODES, axis=1)
+    factor = jnp.concatenate([factor] * 2, axis=0)
+    back_half = left_mul(ah[...], al[...], far * factor)
+    lhs = jnp.concatenate(
+        [jnp.concatenate([back_half[:N, m * N:(m + 1) * N], back_half[N:, m * N:(m + 1) * N]], axis=1)
+         for m in range(MODES)], axis=0)
+    change = right_mul(lhs, bh[...], bl[...])
+    tr = jnp.zeros((N, N), jnp.float32)
+    ti = jnp.zeros((N, N), jnp.float32)
+
+    def accumulate(k, value):
+        if not first:
+            gout[k] += value
+        elif gin is None:
+            gout[k] = value
+        else:
+            gout[k] = gin[k] + value
+
+    for m in range(MODES):
+        qr, qi = probe[0, m], probe[1, m]
+        cr, ci = change[m * N:(m + 1) * N, :N], change[m * N:(m + 1) * N, N:]
+        tr += qr * cr + qi * ci
+        ti += qr * ci - qi * cr
+        accumulate(m, pr * cr + pi * ci)
+        accumulate(MODES + m, pr * ci - pi * cr)
+    accumulate(2 * MODES, pr * pr + pi * pi)
+    return tr, ti
+
+
+def transforms(batch, offs, tiles, probe, amp, gout, gin, z, fixed, tabs):
     lane = lanes((N, N))
-
-    def step(p, carry):
-        r0 = offs[1, 1, 0, batch * 8 + p * 2] + HALF
-        c0 = offs[1, 1, 0, batch * 8 + p * 2 + 1] + HALF
-        t = lax.shift_right_arithmetic(c0, 7)
-        s = lax.bitwise_and(c0, 127)
+    for p, at, t in STATIC:
+        pr, pi = tiles[0, t, at:at + N], tiles[1, t, at:at + N]
+        tr, ti = terms(pr, pi, probe, amp[batch, p], gout, gin, p == 0, *tabs)
+        fixed[p, 0] = tr
+        fixed[p, 1] = ti
+    for n, p in enumerate(MOVING):
+        r0, t, s = spot(offs, (1, 1), batch, p)
         rows = pl.ds(r0, N)
         back = lax.bitwise_and(128 - s, 127)
         after = jnp.minimum(t + 1, 2)
@@ -270,72 +339,56 @@
             two = pltpu.roll(tiles[ch, after, rows], back, 1)
             return jnp.where(lane < 128 - s, one, two)
 
-        pr, pi = cut(0), cut(1)
-        waves = []
-        for m in range(MODES):
-            qr, qi = probe[0, m], probe[1, m]
-            waves.append(jnp.concatenate([qr * pr - qi * pi, qr * pi + qi * pr], axis=1))
-        half = right_mul(jnp.concatenate(waves, axis=0), a3r[...])
-        rows_of = [half[m * N:(m + 1) * N] for m in range(MODES)]
-        stacked = jnp.concatenate(
-            [jnp.concatenate([h[:, :N] for h in rows_of], axis=1),
-             jnp.concatenate([h[:, N:] for h in rows_of], axis=1)], axis=0)
-        far = left_mul(b3l[...], stacked)
-        inten = jnp.zeros((N, N), jnp.float32)
-        for m in range(MODES):
-            fr, fi = far[:N, m * N:(m + 1) * N], far[N:, m * N:(m + 1) * N]
-            inten += fr * fr + fi * fi
-        factor = amp[batch, p] * lax.rsqrt(jnp.maximum(inten, AMP_FLOOR * AMP_FLOOR)) - 1.0
-        factor = jnp.concatenate([factor] * MODES, axis=1)
-        factor = jnp.concatenate([factor] * 2, axis=0)
-        back_half = left_mul(a3l[...], far * factor)
-        lhs = jnp.concatenate(
-            [jnp.concatenate([back_half[:N, m * N:(m + 1) * N], back_half[N:, m * N:(m + 1) * N]], axis=1)
-             for m in range(MODES)], axis=0)
-        change = right_mul(lhs, b3r[...])
-        tr = jnp.zeros((N, N), jnp.float32)
-        ti = jnp.zeros((N, N), jnp.float32)
-        for m in range(MODES):
-            qr, qi = probe[0, m], probe[1, m]
-            cr, ci = change[m * N:(m + 1) * N, :N], change[m * N:(m + 1) * N, N:]
-            tr += qr * cr + qi * ci
-            ti += qr * ci - qi * cr
-            gout[m] += pr * cr + pi * ci
-            gout[MODES + m] += pr * ci - pi * cr
-        gout[2 * MODES] += pr * pr + pi * pi
-        spread(z.at[p, 0], tr, s)
-        spread(z.at[p, 1], ti, s)
-        return carry
-
-    lax.fori_loop(0, POS, step, 0)
+        tr, ti = terms(cut(0), cut(1), probe, amp[batch, p], gout, gin, False, *tabs)
+        spread(z.at[n, 0], tr, s)
+        spread(z.at[n, 1], ti, s)
 
 
 def light_maps(batch, offs, probe, zl, light):
+    row, rows = lax.axis_index("row"), lax.axis_size("row")
+    col, cols = lax.axis_index("col"), lax.axis_size("col")
     lane = lanes((N, N))
     total = jnp.zeros((N, N), jnp.float32)
     for m in range(MODES):
         total += probe[0, m] * probe[0, m] + probe[1, m] * probe[1, m]
-    for j in range(2):
-        zl[j, 0:N] = jnp.zeros((N, N), jnp.float32)
-        zl[j, 2 * N:] = jnp.zeros((N, N), jnp.float32)
-    zl[2, 0:N] = total
-    light[...] = jnp.zeros(light.shape, jnp.float32)
-
-    def step(i, carry):
-        block, p = i // POS, i % POS
-        cr, rr = block // 3, block % 3
-        r0 = offs[cr, rr, 0, batch * 8 + p * 2] + (rr - 1) * TILE + HALF
-        c0 = offs[cr, rr, 0, batch * 8 + p * 2 + 1] + (cr - 1) * TILE + HALF
-        t = lax.shift_right_arithmetic(c0, 7)
-        spread(zl, zl[2, 0:N], lax.bitwise_and(c0, 127))
-        for b in range(3):
-            w = slice(b * N, b * N + N)
-            light[0, w] += window(zl, r0, t, b, 1)
-            light[1, w] += jnp.where(lane < HALF, window(zl, r0, t, b, 2), window(zl, r0, t, b, 0))
-        return carry
-
-    lax.fori_loop(0, 9 * POS, step, 0)
-    row, rows = lax.axis_index("row"), lax.axis_size("row")
+    blank = jnp.zeros((N, N), jnp.float32)
+    slots = zl.shape[0]
+    for n in range(slots):
+        for j in range(2):
+            zl[n, j, 0:N] = blank
+            zl[n, j, 2 * N:] = blank
+
+    def there(yes):
+        return yes.astype(jnp.float32)
+
+    up, down, left, right = there(row > 0), there(row < rows - 1), there(col > 0), there(col < cols - 1)
+    corner = {(0, 0): 1.0 + up * left, (0, 2): right + up, (2, 0): down + left, (2, 2): 1.0 + down * right}
+    sums = {}
+    for i in (0, 2):
+        sums[i] = total * jnp.where(lane < HALF, corner[i, 2], corner[i, 0])
+    light[1, 0:N] = sums[0]
+    light[1, N:2 * N] = blank
+    light[1, 2 * N:] = sums[2]
+    for i in range(3):
+        light[0, i * N:i * N + N] = blank
+
+    n = 0
+    for cr in range(3):
+        for rr in range(3):
+            for p in MOVING:
+                r0, t, s = spot(offs, (cr, rr), batch, p)
+                buf = zl.at[n % slots]
+                n += 1
+                spread(buf, total, s)
+                for i in {0: (0,), 1: (0, 1, 2), 2: (2,)}[rr]:
+                    w = slice(i * N, i * N + N)
+                    if cr == 0:
+                        light[1, w] += jnp.where(lane < HALF, 0.0, window(buf, r0, t, i, 0))
+                    elif cr == 2:
+                        light[1, w] += jnp.where(lane < HALF, window(buf, r0, t, i, 2), 0.0)
+                    else:
+                        light[0, w] += window(buf, r0, t, i, 1)
+                        light[1, w] += jnp.where(lane < HALF, window(buf, r0, t, i, 2), window(buf, r0, t, i, 0))
     place = lax.broadcasted_iota(jnp.int32, (PADROWS, N), 0)
     low = jnp.where(row == 0, HALF, 0)
     high = jnp.where(row == rows - 1, HALF + TILE, PADROWS)
@@ -447,14 +500,18 @@
             pltpu.SemaphoreType.DMA((25,)), pltpu.SemaphoreType.DMA((25,))]
 
 
-def batch_kernel(batch, last, offs, tiles, probe, amp, gin, a3r, b3l, a3l, b3r, *rest):
+def batch_kernel(batch, last, offs, tiles, *rest):
+    tabs, (amp, probe), rest = rest[:4], rest[4:6], rest[6:]
+    gin = None
+    if batch:
+        gin, *rest = rest
     if last:
-        out, step_out, gout, flat, z, zl, light, ls, rs, ls_in, rs_in, me, fresh, from_up, from_down, send, recv, *more = rest
+        out, step_out, gout, flat, z, fixed, zl, light, ls, rs, ls_in, rs_in, me, fresh, from_up, from_down, send, recv, *more = rest
         reach = HALF
         red = Reduction(flat, step_out, *more)
         others = red.peers
     else:
-        out, gout, z, zl, light, ls, rs, ls_in, rs_in, me, fresh, from_up, from_down, sl, sr, hl, hr, send, recv = rest
+        out, gout, z, fixed, zl, light, ls, rs, ls_in, rs_in, me, fresh, from_up, from_down, sl, sr, hl, hr, send, recv = rest
         reach = N
         others = ()
     up, down, left, right = sides = position()
@@ -464,20 +521,14 @@
     greet(sides, others)
 
     blank = jnp.zeros((N, N), jnp.float32)
-    for p in range(POS):
+    for n in range(len(MOVING)):
         for ch in range(2):
             for j in range(2):
-                z[p, ch, j, 0:N] = blank
-                z[p, ch, j, 2 * N:] = blank
-    gout[...] = gin[...]
-    transforms(batch, offs, tiles, probe, amp, gout, z, a3r, b3l, a3l, b3r)
+                z[n, ch, j, 0:N] = blank
+                z[n, ch, j, 2 * N:] = blank
+    transforms(batch, offs, tiles, probe, amp, gout, gin, z, fixed, tabs)
     if last:
         flat[...] = gout[...].reshape(TILES, 8, N)
-    spots = []
-    for p in range(POS):
-        r0 = offs[1, 1, 0, batch * 8 + p * 2] + HALF
-        c0 = offs[1, 1, 0, batch * 8 + p * 2 + 1] + HALF
-        spots.append((p, r0, lax.shift_right_arithmetic(c0, 7)))
     greeted(sides, others)
 
     count = iter(range(100))
@@ -488,9 +539,13 @@
 
     def gathered(ch, i, k):
         acc = None
-        for p, r0, t in spots:
-            w = window(z.at[p, ch], r0, t, i, k)
+        for n, p in enumerate(MOVING):
+            r0, t, _ = spot(offs, (1, 1), batch, p)
+            w = window(z.at[n, ch], r0, t, i, k)
             acc = w if acc is None else acc + w
+        for p, at, tile in STATIC:
+            if (at, tile) == (i * N, k):
+                acc = acc + fixed[p, ch]
         return acc
 
     lane = lanes((N, N))
@@ -623,7 +678,7 @@
         c.sent()
 
 
-def run_batch(batch, last, offs, tiles, probe, amp, gin, tabs):
+def run_batch(batch, last, offs, tiles, others, gin):
     f = jnp.float32
     strip = pltpu.VMEM((PADROWS, N), f)
     sums = jax.ShapeDtypeStruct((2 * MODES + 1, N, N), f)
@@ -637,11 +692,12 @@
     return pl.pallas_call(
         functools.partial(batch_kernel, batch, last),
         out_shape=shapes,
-        in_specs=[SM] + [VM] * 8,
+        in_specs=[SM] + [VM] * (1 + len(others) + len(gin)),
         out_specs=(VM,) * len(shapes),
         scratch_shapes=extra + [
-            pltpu.VMEM((POS, 2, 2, PADROWS, N), f),
-            pltpu.VMEM((3, PADROWS, N), f),
+            pltpu.VMEM((len(MOVING), 2, 2, PADROWS, N), f),
+            pltpu.VMEM((len(STATIC), 2, N, N), f),
+            pltpu.VMEM((3, 2, PADROWS, N), f),
             pltpu.VMEM((2, PADROWS, N), f),
             strip, strip, strip, strip,
             pltpu.VMEM((2, 2, PADROWS, N), f),
@@ -655,18 +711,20 @@
         compiler_params=pltpu.CompilerParams(
             collective_id=1 + batch, has_side_effects=True, vmem_limit_bytes=36 * 2**20),
         name=f"batch{batch}",
-    )(offs, tiles, probe, amp, gin, *tabs)
+    )(offs, tiles, *others, *gin)
 
 
 def on_device(object_field, probe, amplitudes, offsets):
     mine = jnp.pad(offsets.reshape(1, 24), ((0, 7), (0, N - 24)))
+    amps = amplitudes.reshape(BATCHES, POS, N, N)
     tabs = [jnp.asarray(t) for t in tables()]
-    tiles, offs = run_first(object_field, mine)
-    grads = jnp.zeros((2 * MODES + 1, N, N), jnp.float32)
-    amps = amplitudes.reshape(BATCHES, POS, N, N)
+    keep = lambda a: pltpu.with_memory_space_constraint(a, pltpu.HBM)
+    tiles, offs, *others = run_first(keep(object_field), mine, [keep(a) for a in (*tabs, amps, probe)])
+    grads = ()
     for b in range(BATCHES - 1):
-        tiles, grads = run_batch(b, False, offs, tiles, probe, amps, grads, tabs)
-    obj, step = run_batch(BATCHES - 1, True, offs, tiles, probe, amps, grads, tabs)
+        tiles, sums = run_batch(b, False, offs, tiles, others, grads)
+        grads = (sums,)
+    obj, step = run_batch(BATCHES - 1, True, offs, tiles, others, grads)
     return obj, step.reshape(2, MODES, N, N)
 
 

time: 136 us -> 123 us (0.904)
  local copies, waits for them, and re-layouts: 8.65 us -> 2.47 us
  Pallas kernels: 126 us -> 120 us
    pallas_call x3, Pallas kernels: 109 us -> 103 us  [run_batch(): pl.pallas_call(functools.partial(batch_kernel, batch, last), out_shape=sh...]
    unnamed x25 -> x3, local copies, waits for them, and re-layouts: 8.52 us -> 2.37 us
where the time goes in v3:
time: 123 us
  Pallas kernels  120 us (98%)
  local copies, waits for them, and re-layouts  2.47 us (2%)
    pallas_call x3, Pallas kernels, run_batch(): pl.pallas_call(functools.partial(batch_kernel, batch, last), out_shape=sh...  103 us
    pallas_call x1, Pallas kernels, run_first(): pl.pallas_call(first_kernel, out_shape=(jax.ShapeDtypeStruct((2, 3, PADRO...  17.4 us

profile of v3, /device:TPU:1, one launch (start us, length us, event | category | flops | bytes accessed | tf_op | source)
XLA Modules:
  0.0 123.4 jit_solution(7417200743539450615)
XLA Ops:
  0.6 0.8 copy.11
  1.4 0.1 reshape.13
  1.5 17.4 %first.1 = (f32[2,3,384,128]{3,2,1,0:T(8,128)S(1)}, s32[3,3,8,128]{3,2,1,0:T(8,128)S(1)}, bf16[256,256]{1,0:T(8,128)(2,1)S(1)}, bf16[256,256]{1,0:T(8,128)(2,1)S...) custom-call(f32[2,256,256]{2,1,0:T(8,128)} %obj_hbm.1, ...), custom_call_target="tpu_custom_call" | custom-call | tf_op jit(solution)/shard_map/first/pallas_call | solution.py:232
  18.9 29.4 %batch0.1 = (f32[2,3,384,128]{3,2,1,0:T(8,128)S(1)}, f32[9,128,128]{2,1,0:T(8,128)S(1)}) custom-call(s32[3,3,8,128]{3,2,1,0:T(8,128)S(1)} %get-tuple-element.16.offs, f32[2,3,384,128]{3,2,1,0:T(8,128)S(1)} %get-tuple-element.17.tiles, bf16[256,256]{1,0:T(8,128)(2,1)S(1)} %get-tuple-element.18.rest_0_, bf16[256,256]{1,0:T(8,128)(2,1)S(1)} %get-tuple-element.19.rest_1_, ...), custom_call_target="tpu_custom_call" | custom-call | tf_op jit(solution)/shard_map/batch0/pallas_call | solution.py:692
  48.4 24.8 %batch1.1 = (f32[2,3,384,128]{3,2,1,0:T(8,128)S(1)}, f32[9,128,128]{2,1,0:T(8,128)S(1)}) custom-call(s32[3,3,8,128]{3,2,1,0:T(8,128)S(1)} %get-tuple-element.16.offs, f32[2,3,384,128]{3,2,1,0:T(8,128)S(1)} %get-tuple-element.24.tiles, bf16[256,256]{1,0:T(8,128)(2,1)S(1)} %get-tuple-element.18.rest_0_, bf16[256,256]{1,0:T(8,128)(2,1)S(1)} %get-tuple-element.19.rest_1_, ...), custom_call_target="tpu_custom_call" | custom-call | tf_op jit(solution)/shard_map/batch1/pallas_call | solution.py:692
  73.2 48.6 %batch2.1 = (f32[2,256,256]{2,1,0:T(8,128)S(1)}, f32[128,8,128]{2,1,0:T(8,128)S(1)}) custom-call(s32[3,3,8,128]{3,2,1,0:T(8,128)S(1)} %get-tuple-element.16.offs, f32[2,3,384,128]{3,2,1,0:T(8,128)S(1)} %get-tuple-element.26.tiles, bf16[256,256]{1,0:T(8,128)(2,1)S(1)} %get-tuple-element.18.rest_0_, bf16[256,256]{1,0:T(8,128)(2,1)S(1)} %get-tuple-element.19.rest_1_, ...), custom_call_target="tpu_custom_call" | custom-call | tf_op jit(solution)/shard_map/batch2/pallas_call | solution.py:692
  121.8 0.8 copy.14
  122.6 0.8 copy.15
  (1 shorter events, 0.0 us)

commit v4 on v3

--- a/solution.py
+++ b/solution.py
@@ -321,13 +321,8 @@
     return tr, ti
 
 
-def transforms(batch, offs, tiles, probe, amp, gout, gin, z, fixed, tabs):
+def moving_terms(batch, offs, tiles, probe, amp, gout, gin, z, tabs):
     lane = lanes((N, N))
-    for p, at, t in STATIC:
-        pr, pi = tiles[0, t, at:at + N], tiles[1, t, at:at + N]
-        tr, ti = terms(pr, pi, probe, amp[batch, p], gout, gin, p == 0, *tabs)
-        fixed[p, 0] = tr
-        fixed[p, 1] = ti
     for n, p in enumerate(MOVING):
         r0, t, s = spot(offs, (1, 1), batch, p)
         rows = pl.ds(r0, N)
@@ -339,9 +334,17 @@
             two = pltpu.roll(tiles[ch, after, rows], back, 1)
             return jnp.where(lane < 128 - s, one, two)
 
-        tr, ti = terms(cut(0), cut(1), probe, amp[batch, p], gout, gin, False, *tabs)
+        tr, ti = terms(cut(0), cut(1), probe, amp[batch, p], gout, gin, n == 0, *tabs)
         spread(z.at[n, 0], tr, s)
         spread(z.at[n, 1], ti, s)
+
+
+def static_terms(batch, tiles, probe, amp, gout, fixed, tabs):
+    for p, at, t in STATIC:
+        pr, pi = tiles[0, t, at:at + N], tiles[1, t, at:at + N]
+        tr, ti = terms(pr, pi, probe, amp[batch, p], gout, None, False, *tabs)
+        fixed[p, 0] = tr
+        fixed[p, 1] = ti
 
 
 def light_maps(batch, offs, probe, zl, light):
@@ -399,105 +402,119 @@
 
 TILES = 144
 HALFT = 72
-PIECE = 9
-SUB = 3
-
-
-class Reduction:
-    def __init__(self, g, out, r1, s1, r2, s2, r3, z, fin, ag1, ag2, ag3, send, recv):
-        self.refs = (g, out, r1, s1, r2, s2, r3, z, fin, ag1, ag2, ag3)
-        self.send, self.recv = send, recv
-        self.count = iter(range(100))
-        self.every = []
-        row, col = lax.axis_index("row"), lax.axis_index("col")
-        self.x, self.zh = row // 4, row % 4
-        self.core, self.group = col % 2, col // 2
-        self.row, self.col = row, col
-        self.partner = {"row": row, "col": col + 1 - 2 * self.core}
-        self.peers = [self.partner]
-        self.peers += [self.group_dev(self.in_group(d)) for d in range(1, 8)]
-        self.peers += [self.x_dev(d) for d in range(1, 4)]
-        self.peers += [self.z_dev(d) for d in range(1, 4)]
-
-    def in_group(self, d):
-        return lax.rem(self.group + d, 8)
-
-    def group_dev(self, k):
-        return {"row": self.row, "col": k * 2 + self.core}
-
-    def x_dev(self, d):
-        return {"row": lax.rem(self.x + d, 4) * 4 + self.zh, "col": self.col}
-
-    def z_dev(self, d):
-        return {"row": self.x * 4 + lax.rem(self.zh + d, 4), "col": self.col}
-
-    def go(self, src, dst, device):
-        i = next(self.count)
+PART = 36
+SPLITS = (("group", 8, 5, "x", 4, 2), ("x", 4, 9, "group", 8, 2))
+
+
+class Mates:
+    def __init__(self):
+        self.row, self.col = lax.axis_index("row"), lax.axis_index("col")
+        self.x, self.zh = self.row // 4, self.row % 4
+        self.core, self.group = self.col % 2, self.col // 2
+        self.partner = {"row": self.row, "col": self.col + 1 - 2 * self.core}
+
+    def at(self, axis, d):
+        if axis == "group":
+            k = lax.rem(self.group + d, 8)
+            return k, {"row": self.row, "col": k * 2 + self.core}
+        if axis == "x":
+            k = lax.rem(self.x + d, 4)
+            return k, {"row": k * 4 + self.zh, "col": self.col}
+        k = lax.rem(self.zh + d, 4)
+        return k, {"row": self.x * 4 + k, "col": self.col}
+
+    def everyone(self):
+        return ([self.partner] + [self.at("group", d)[1] for d in range(1, 8)]
+                + [self.at("x", d)[1] for d in range(1, 4)] + [self.at("z", d)[1] for d in range(1, 4)])
+
+
+def reduce_part(part, mates, g, whole, bufs):
+    axis1, n1, p1, axis2, n2, p2 = SPLITS[part]
+    r1, s1, r2, s2, r3, z, fin, ag1, ag2, send, recv = bufs
+    count = iter(range(100))
+    every = []
+
+    def go(src, dst, device):
+        i = next(count)
         c = pltpu.make_async_remote_copy(
-            src_ref=src, dst_ref=dst, send_sem=self.send.at[i], recv_sem=self.recv.at[i],
+            src_ref=src, dst_ref=dst, send_sem=send.at[i], recv_sem=recv.at[i],
             device_id=device, device_id_type=MESH)
         c.start()
-        self.every.append(c)
+        every.append(c)
         return c
 
-    def stages(self):
-        g, out, r1, s1, r2, s2, r3, z, fin, ag1, ag2, ag3 = self.refs
-        x, zh, core, group, go, in_group = self.x, self.zh, self.core, self.group, self.go, self.in_group
-        s2[pl.ds(PIECE, 12 - PIECE)] = jnp.zeros((12 - PIECE, 8, N), jnp.float32)
-        c = go(g.at[pl.ds((1 - core) * HALFT, HALFT)], r1, self.partner)
-        yield
-        c.wait_recv()
-        s1[...] = g[pl.ds(core * HALFT, HALFT)] + r1[...]
-        cs = [go(s1.at[pl.ds(in_group(d) * PIECE, PIECE)], r2.at[d - 1], self.group_dev(in_group(d))) for d in range(1, 8)]
-        yield
-        acc = s1[pl.ds(group * PIECE, PIECE)]
+    def scatter(src, slots, axis, n, p):
+        cs = []
+        for d in range(1, n):
+            k, device = mates.at(axis, d)
+            cs.append(go(src.at[pl.ds(k * p, p)], slots.at[d - 1], device))
+        return cs
+
+    def collect(src, slots, axis, p, cs):
+        acc = src[pl.ds(mates.at(axis, 0)[0] * p, p)]
         for d, c in enumerate(cs):
             c.wait_recv()
-            acc = acc + r2[d]
-        s2[pl.ds(0, PIECE)] = acc
-        cs = [go(s2.at[pl.ds(lax.rem(x + d, 4) * SUB, SUB)], r3.at[d - 1], self.x_dev(d)) for d in range(1, 4)]
-        yield
-        acc = s2[pl.ds(x * SUB, SUB)]
-        for d, c in enumerate(cs):
-            c.wait_recv()
-            acc = acc + r3[d]
-        z[0] = acc
-        cs = [go(z.at[0], z.at[d], self.z_dev(d)) for d in range(1, 4)]
-        yield
-        for c in cs:
-            c.wait_recv()
-        acc = z[lax.rem(zh, 4)]
-        for k in range(1, 4):
-            acc = acc + z[lax.rem(zh - k + 4, 4)]
-        fin[...] = acc
-        cs = [go(fin, ag1.at[pl.ds(x * SUB, SUB)], self.x_dev(d)) for d in range(1, 4)]
-        ag1[pl.ds(x * SUB, SUB)] = fin[...]
-        yield
-        for c in cs:
-            c.wait_recv()
-        cs = [go(ag1.at[pl.ds(0, PIECE)], ag2.at[pl.ds(group * PIECE, PIECE)], self.group_dev(in_group(d))) for d in range(1, 8)]
-        ag2[pl.ds(group * PIECE, PIECE)] = ag1[pl.ds(0, PIECE)]
-        yield
-        for c in cs:
-            c.wait_recv()
-        c = go(ag2, ag3.at[pl.ds(core * HALFT, HALFT)], self.partner)
-        ag3[pl.ds(core * HALFT, HALFT)] = ag2[...]
-        yield
+            acc = acc + slots[d]
+        return acc
+
+    def gather(src, dst, axis, n, p):
+        me = pl.ds(mates.at(axis, 0)[0] * p, p)
+        cs = [go(src, dst.at[me], mates.at(axis, d)[1]) for d in range(1, n)]
+        dst[me] = src[...]
+        return cs
+
+    core = mates.core
+    if s1.shape[0] > PART:
+        s1[pl.ds(PART, s1.shape[0] - PART)] = jnp.zeros((s1.shape[0] - PART, 8, N), jnp.float32)
+    s2[pl.ds(p1, s2.shape[0] - p1)] = jnp.zeros((s2.shape[0] - p1, 8, N), jnp.float32)
+    c = go(g.at[pl.ds((1 - core) * HALFT + part * PART, PART)], r1, mates.partner)
+    yield
+    c.wait_recv()
+    s1[pl.ds(0, PART)] = g[pl.ds(core * HALFT + part * PART, PART)] + r1[...]
+    cs = scatter(s1, r2, axis1, n1, p1)
+    yield
+    s2[pl.ds(0, p1)] = collect(s1, r2, axis1, p1, cs)
+    cs = scatter(s2, r3, axis2, n2, p2)
+    yield
+    z[0] = collect(s2, r3, axis2, p2, cs)
+    cs = [go(z.at[0], z.at[d], mates.at("z", d)[1]) for d in range(1, 4)]
+    yield
+    for c in cs:
         c.wait_recv()
-        inv = lax.rsqrt(ag3[pl.ds(128, 16)] + PROBE_REG)
-        for k in range(8):
-            out[pl.ds(16 * k, 16)] = ag3[pl.ds(16 * k, 16)] * inv
-        for c in self.every:
-            c.wait_send()
-        yield
+    acc = z[lax.rem(mates.zh, 4)]
+    for k in range(1, 4):
+        acc = acc + z[lax.rem(mates.zh - k + 4, 4)]
+    fin[...] = acc
+    cs = gather(fin, ag1, axis2, n2, p2)
+    yield
+    for c in cs:
+        c.wait_recv()
+    cs = gather(ag1.at[pl.ds(0, p1)], ag2, axis1, n1, p1)
+    yield
+    for c in cs:
+        c.wait_recv()
+    mine = pl.ds(core * HALFT + part * PART, PART)
+    c = go(ag2.at[pl.ds(0, PART)], whole.at[mine], mates.partner)
+    whole[mine] = ag2[pl.ds(0, PART)]
+    yield
+    c.wait_recv()
+    for c in every:
+        c.wait_send()
+    yield
+
+
+PART_REFS = 11
 
 
 def reduction_scratch():
     f = jnp.float32
     shape = lambda *n: pltpu.VMEM(n + (8, N), f)
-    return [shape(HALFT), shape(HALFT), shape(7, PIECE), shape(12), shape(3, SUB),
-            shape(4, SUB), shape(SUB), shape(12), shape(HALFT), shape(TILES),
-            pltpu.SemaphoreType.DMA((25,)), pltpu.SemaphoreType.DMA((25,))]
+    refs = [shape(TILES)]
+    for _, n1, p1, _, n2, p2 in SPLITS:
+        refs += [shape(PART), shape(n1 * p1), shape(n1 - 1, p1), shape(n2 * p2), shape(n2 - 1, p2),
+                 shape(4, p2), shape(p2), shape(n2 * p2), shape(n1 * p1),
+                 pltpu.SemaphoreType.DMA((25,)), pltpu.SemaphoreType.DMA((25,))]
+    return refs
 
 
 def batch_kernel(batch, last, offs, tiles, *rest):
@@ -505,20 +522,25 @@
     gin = None
     if batch:
         gin, *rest = rest
+    others, parts = (), ()
     if last:
-        out, step_out, gout, flat, z, fixed, zl, light, ls, rs, ls_in, rs_in, me, fresh, from_up, from_down, send, recv, *more = rest
+        out, step_out, gout, flat, z, fixed, zl, light, ls, rs, ls_in, rs_in, me, fresh, from_up, from_down, send, recv, whole, *more = rest
+        mates = Mates()
+        others = mates.everyone()
+        parts = [reduce_part(k, mates, flat, whole, more[k * PART_REFS:(k + 1) * PART_REFS]) for k in range(2)]
         reach = HALF
-        red = Reduction(flat, step_out, *more)
-        others = red.peers
     else:
         out, gout, z, fixed, zl, light, ls, rs, ls_in, rs_in, me, fresh, from_up, from_down, sl, sr, hl, hr, send, recv = rest
         reach = N
-        others = ()
     up, down, left, right = sides = position()
     clear_missing([(left[0], rs_in), (right[0], ls_in), (up[0], from_up), (down[0], from_down)])
     if not last:
         clear_missing([(left[0], hl), (right[0], hr)])
     greet(sides, others)
+
+    def advance():
+        for part in parts:
+            next(part)
 
     blank = jnp.zeros((N, N), jnp.float32)
     for n in range(len(MOVING)):
@@ -526,16 +548,18 @@
             for j in range(2):
                 z[n, ch, j, 0:N] = blank
                 z[n, ch, j, 2 * N:] = blank
-    transforms(batch, offs, tiles, probe, amp, gout, gin, z, fixed, tabs)
-    if last:
-        flat[...] = gout[...].reshape(TILES, 8, N)
+    moving_terms(batch, offs, tiles, probe, amp, gout, gin, z, tabs)
     greeted(sides, others)
 
     count = iter(range(100))
+    every = []
 
     def link(src, dst, to, source):
         i = next(count)
-        return Link(src, dst, send.at[i], recv.at[i], to, source)
+        c = Link(src, dst, send.at[i], recv.at[i], to, source)
+        c.start()
+        every.append(c)
+        return c
 
     def gathered(ch, i, k):
         acc = None
@@ -549,10 +573,10 @@
         return acc
 
     lane = lanes((N, N))
-    every = []
     cols = {}
-
-    def send_cols(i):
+    row_links = {}
+
+    def side_strips(i):
         w = slice(i * N, i * N + N)
         t0 = [gathered(ch, i, 0) for ch in range(2)]
         t2 = [gathered(ch, i, 2) for ch in range(2)]
@@ -560,61 +584,60 @@
         rs[w] = jnp.where(lane < HALF, turn(t2[0]), t2[1])
         for ch in range(2):
             me[1, ch, w] = jnp.where(lane < HALF, t2[ch], t0[ch])
-        d = pl.ds(i * N, N)
-        cols[i] = [link(ls.at[d], ls_in.at[d], left, right), link(rs.at[d], rs_in.at[d], right, left)]
-        for c in cols[i]:
-            c.start()
-        every.extend(cols[i])
+
+    def send_cols(at, size):
+        d = pl.ds(at, size)
+        cols[at] = [link(ls.at[d], ls_in.at[d], left, right), link(rs.at[d], rs_in.at[d], right, left)]
 
     def middle(i):
         for ch in range(2):
             me[0, ch, i * N:i * N + N] = gathered(ch, i, 1)
 
-    def fold_cols(i):
-        for c in cols[i]:
+    def send_rows(which, top, at, size):
+        base = 0 if top else PADROWS - reach
+        src, dst = pl.ds(at, size), pl.ds(at - base, size)
+        if top:
+            c = link(me.at[which, :, src, :], from_down.at[which, :, dst, :], up, down)
+        else:
+            c = link(me.at[which, :, src, :], from_up.at[which, :, dst, :], down, up)
+        row_links[which, top, at - base] = c
+
+    def fold_cols(at, size):
+        for c in cols[at]:
             c.arrived()
-        w = slice(i * N, i * N + N)
+        w = slice(at, at + size)
+        side = lanes((size, N))
         a, b = ls_in[w], rs_in[w]
-        me[1, 0, w] += jnp.where(lane < HALF, a, turn(b))
-        me[1, 1, w] += jnp.where(lane < HALF, turn(a), b)
-
-    stage = iter(red.stages()) if last else iter([None] * 20)
-    next(stage)
-    send_cols(0)
-    send_cols(2)
+        me[1, 0, w] += jnp.where(side < HALF, a, turn(b))
+        me[1, 1, w] += jnp.where(side < HALF, turn(a), b)
+
     middle(0)
-    row_links = {}
-
-    def rows_pair(which, top):
-        if last:
-            at = 0 if top else PADROWS - HALF
-        else:
-            at = 0 if top else PADROWS - N
-        d = pl.ds(at, reach)
-        if top:
-            c = link(me.at[which, :, d, :], from_down.at[which], up, down)
-        else:
-            c = link(me.at[which, :, d, :], from_up.at[which], down, up)
-        c.start()
-        every.append(c)
-        row_links[which, top] = c
-
-    rows_pair(0, True)
+    send_rows(0, True, 0, reach)
     middle(2)
-    rows_pair(0, False)
-    send_cols(1)
+    send_rows(0, False, PADROWS - reach, reach)
+    side_strips(1)
+    send_cols(N, N)
+    static_terms(batch, tiles, probe, amp, gout, fixed, tabs)
+    if last:
+        flat[...] = gout[...].reshape(TILES, 8, N)
+    advance()
+    order = ((0, True), (320, False), (64, True), (256, False))
+    for i in (0, 2):
+        side_strips(i)
+        if i == 0:
+            send_cols(0, HALF)
+    send_cols(320, HALF)
+    send_cols(64, HALF)
+    send_cols(256, HALF)
+    advance()
     middle(1)
-    if last:
-        next(stage)
     light_maps(batch, offs, probe, zl, light)
-    fold_cols(0)
-    rows_pair(1, True)
-    fold_cols(2)
-    rows_pair(1, False)
-    fold_cols(1)
-    if last:
-        next(stage)
-
+    for at, top in order:
+        fold_cols(at, HALF)
+        if not last or at in (0, 320):
+            send_rows(1, top, at, HALF)
+    advance()
+    fold_cols(N, N)
     halos = []
 
     def update(which, at, size, extra):
@@ -624,51 +647,54 @@
         for ch in range(2):
             t = me[which, ch, w]
             if extra is not None:
-                t = t + extra[which, ch]
+                t = t + extra[ch]
             old = tiles[ch, 1, w] if which == 0 else jnp.where(mine < HALF, tiles[ch, 2, w], tiles[ch, 0, w])
             fresh[which, ch, w] = old + t * lv
 
     def halo(at, size):
+        if last:
+            return
         w = slice(at, at + size)
         a, b = halo_strips(fresh[1, 0, w], fresh[1, 1, w])
         sl[w] = a
         sr[w] = b
         d = pl.ds(at, size)
-        both = [link(sl.at[d], hr.at[d], left, right), link(sr.at[d], hl.at[d], right, left)]
-        for c in both:
-            c.start()
-        halos.extend(both)
+        halos.extend([link(sl.at[d], hr.at[d], left, right), link(sr.at[d], hl.at[d], right, left)])
 
     update(1, N, N, None)
-    if not last:
-        halo(N, N)
+    halo(N, N)
     update(0, N, N, None)
+    advance()
     if last:
-        next(stage)
-    start = HALF if last else 0
-    row_links[1, False].arrived()
-    update(1, start, reach, from_up)
-    if not last:
-        halo(0, N)
-    row_links[1, True].arrived()
-    update(1, 2 * N, reach, from_down)
-    if not last:
-        halo(2 * N, N)
-    row_links[0, False].arrived()
-    update(0, start, reach, from_up)
-    row_links[0, True].arrived()
-    update(0, 2 * N, reach, from_down)
-    every.extend(halos)
-    if last:
+        row_links[1, False, 0].arrived()
+        update(1, HALF, HALF, from_up.at[1])
+        row_links[1, True, 0].arrived()
+        update(1, 256, HALF, from_down.at[1])
+        row_links[0, False, 0].arrived()
+        update(0, HALF, HALF, from_up.at[0])
+        row_links[0, True, 0].arrived()
+        update(0, 256, HALF, from_down.at[0])
         wide = lanes((TILE, N))
         w = slice(HALF, HALF + TILE)
         for ch in range(2):
             m, e = fresh[0, ch, w], fresh[1, ch, w]
             out[ch, :, 0:128] = turn(jnp.where(wide < HALF, m, e))
             out[ch, :, 128:256] = turn(jnp.where(wide < HALF, e, m))
-        for _ in stage:
-            pass
+        for _ in range(4):
+            advance()
+        inv = lax.rsqrt(whole[pl.ds(128, 16)] + PROBE_REG)
+        for k in range(8):
+            step_out[pl.ds(16 * k, 16)] = whole[pl.ds(16 * k, 16)] * inv
     else:
+        for top, at in ((True, 0), (False, 64), (True, 64), (False, 0)):
+            row_links[1, top, at].arrived()
+            source, base = (from_down, 2 * N) if top else (from_up, 0)
+            update(1, base + at, HALF, source.at[1, :, pl.ds(at, HALF), :])
+            halo(base + at, HALF)
+        row_links[0, False, 0].arrived()
+        update(0, 0, N, from_up.at[0])
+        row_links[0, True, 0].arrived()
+        update(0, 2 * N, N, from_down.at[0])
         for ch in range(2):
             out[ch, 1] = fresh[0, ch]
         for c in halos:
@@ -705,8 +731,8 @@
             pltpu.VMEM((2, 2, reach, N), f),
             pltpu.VMEM((2, 2, reach, N), f),
         ] + ([] if last else [strip] * 4) + [
-            pltpu.SemaphoreType.DMA((16,)),
-            pltpu.SemaphoreType.DMA((16,)),
+            pltpu.SemaphoreType.DMA((26,)),
+            pltpu.SemaphoreType.DMA((26,)),
         ] + (reduction_scratch() if last else []),
         compiler_params=pltpu.CompilerParams(
             collective_id=1 + batch, has_side_effects=True, vmem_limit_bytes=36 * 2**20),

time: 123 us -> 117 us (0.951)
  Pallas kernels: 120 us -> 114 us
    pallas_call x3, Pallas kernels: 103 us -> 96.7 us  [run_batch(): pl.pallas_call(functools.partial(batch_kernel, batch, last), out_shape=sh...]
where the time goes in v4:
time: 117 us
  Pallas kernels  114 us (97%)
  local copies, waits for them, and re-layouts  2.47 us (2%)
    pallas_call x3, Pallas kernels, run_batch(): pl.pallas_call(functools.partial(batch_kernel, batch, last), out_shape=sh...  96.7 us
    pallas_call x1, Pallas kernels, run_first(): pl.pallas_call(first_kernel, out_shape=(jax.ShapeDtypeStruct((2, 3, PADRO...  17.4 us
    unnamed x3, local copies, waits for them, and re-layouts  2.37 us

profile of v4, /device:TPU:1, one launch (start us, length us, event | category | flops | bytes accessed | tf_op | source)
XLA Modules:
  0.0 117.2 jit_solution(17761430996421025780)
XLA Ops:
  0.6 0.8 copy.11
  1.4 0.1 reshape.13
  1.5 17.4 %first.1 = (f32[2,3,384,128]{3,2,1,0:T(8,128)S(1)}, s32[3,3,8,128]{3,2,1,0:T(8,128)S(1)}, bf16[256,256]{1,0:T(8,128)(2,1)S(1)}, bf16[256,256]{1,0:T(8,128)(2,1)S...) custom-call(f32[2,256,256]{2,1,0:T(8,128)} %obj_hbm.1, ...), custom_call_target="tpu_custom_call" | custom-call | tf_op jit(solution)/shard_map/first/pallas_call | solution.py:232
  18.9 26.1 %batch0.1 = (f32[2,3,384,128]{3,2,1,0:T(8,128)S(1)}, f32[9,128,128]{2,1,0:T(8,128)S(1)}) custom-call(s32[3,3,8,128]{3,2,1,0:T(8,128)S(1)} %get-tuple-element.16.offs, f32[2,3,384,128]{3,2,1,0:T(8,128)S(1)} %get-tuple-element.17.tiles, bf16[256,256]{1,0:T(8,128)(2,1)S(1)} %get-tuple-element.18.rest_0_, bf16[256,256]{1,0:T(8,128)(2,1)S(1)} %get-tuple-element.19.rest_1_, ...), custom_call_target="tpu_custom_call" | custom-call | tf_op jit(solution)/shard_map/batch0/pallas_call | solution.py:718
  45.0 25.2 %batch1.1 = (f32[2,3,384,128]{3,2,1,0:T(8,128)S(1)}, f32[9,128,128]{2,1,0:T(8,128)S(1)}) custom-call(s32[3,3,8,128]{3,2,1,0:T(8,128)S(1)} %get-tuple-element.16.offs, f32[2,3,384,128]{3,2,1,0:T(8,128)S(1)} %get-tuple-element.24.tiles, bf16[256,256]{1,0:T(8,128)(2,1)S(1)} %get-tuple-element.18.rest_0_, bf16[256,256]{1,0:T(8,128)(2,1)S(1)} %get-tuple-element.19.rest_1_, ...), custom_call_target="tpu_custom_call" | custom-call | tf_op jit(solution)/shard_map/batch1/pallas_call | solution.py:718
  70.2 45.4 %batch2.1 = (f32[2,256,256]{2,1,0:T(8,128)S(1)}, f32[128,8,128]{2,1,0:T(8,128)S(1)}) custom-call(s32[3,3,8,128]{3,2,1,0:T(8,128)S(1)} %get-tuple-element.16.offs, f32[2,3,384,128]{3,2,1,0:T(8,128)S(1)} %get-tuple-element.26.tiles, bf16[256,256]{1,0:T(8,128)(2,1)S(1)} %get-tuple-element.18.rest_0_, bf16[256,256]{1,0:T(8,128)(2,1)S(1)} %get-tuple-element.19.rest_1_, ...), custom_call_target="tpu_custom_call" | custom-call | tf_op jit(solution)/shard_map/batch2/pallas_call | solution.py:718
  115.6 0.8 copy.14
  116.4 0.8 copy.15
  (1 shorter events, 0.0 us)

commit v5 on v4

--- a/solution.py
+++ b/solution.py
@@ -611,32 +611,49 @@
         me[1, 0, w] += jnp.where(side < HALF, a, turn(b))
         me[1, 1, w] += jnp.where(side < HALF, turn(a), b)
 
-    middle(0)
-    send_rows(0, True, 0, reach)
-    middle(2)
-    send_rows(0, False, PADROWS - reach, reach)
-    side_strips(1)
-    send_cols(N, N)
-    static_terms(batch, tiles, probe, amp, gout, fixed, tabs)
+    order = ((0, True), (320, False), (64, True), (256, False))
+
+    def send_edges():
+        for at, top in order:
+            fold_cols(at, HALF)
+            if not last or at in (0, 320):
+                send_rows(1, top, at, HALF)
+
     if last:
+        static_terms(batch, tiles, probe, amp, gout, fixed, tabs)
         flat[...] = gout[...].reshape(TILES, 8, N)
-    advance()
-    order = ((0, True), (320, False), (64, True), (256, False))
-    for i in (0, 2):
-        side_strips(i)
-        if i == 0:
-            send_cols(0, HALF)
-    send_cols(320, HALF)
-    send_cols(64, HALF)
-    send_cols(256, HALF)
-    advance()
-    middle(1)
-    light_maps(batch, offs, probe, zl, light)
-    for at, top in order:
-        fold_cols(at, HALF)
-        if not last or at in (0, 320):
-            send_rows(1, top, at, HALF)
-    advance()
+        advance()
+        middle(0)
+        send_rows(0, True, 0, reach)
+        middle(2)
+        send_rows(0, False, PADROWS - reach, reach)
+        advance()
+        for i in (0, 2, 1):
+            side_strips(i)
+        middle(1)
+        light_maps(batch, offs, probe, zl, light)
+        advance()
+        for at, _ in order:
+            send_cols(at, HALF)
+        send_cols(N, N)
+        advance()
+        send_edges()
+    else:
+        middle(0)
+        send_rows(0, True, 0, reach)
+        middle(2)
+        send_rows(0, False, PADROWS - reach, reach)
+        side_strips(1)
+        send_cols(N, N)
+        static_terms(batch, tiles, probe, amp, gout, fixed, tabs)
+        side_strips(0)
+        send_cols(0, HALF)
+        side_strips(2)
+        for at in (320, 64, 256):
+            send_cols(at, HALF)
+        middle(1)
+        light_maps(batch, offs, probe, zl, light)
+        send_edges()
     fold_cols(N, N)
     halos = []
 
@@ -664,7 +681,6 @@
     update(1, N, N, None)
     halo(N, N)
     update(0, N, N, None)
-    advance()
     if last:
         row_links[1, False, 0].arrived()
         update(1, HALF, HALF, from_up.at[1])

time: 117 us -> 118 us (level)
  no operation moved by 1% of the time
where the time goes in v5:
time: 118 us
  Pallas kernels  115 us (97%)
  local copies, waits for them, and re-layouts  2.47 us (2%)
    pallas_call x3, Pallas kernels, run_batch(): pl.pallas_call(functools.partial(batch_kernel, batch, last), out_shape=sh...  97.4 us
    pallas_call x1, Pallas kernels, run_first(): pl.pallas_call(first_kernel, out_shape=(jax.ShapeDtypeStruct((2, 3, PADRO...  17.4 us
    unnamed x3, local copies, waits for them, and re-layouts  2.37 us

profile of v5, /device:TPU:1, one launch (start us, length us, event | category | flops | bytes accessed | tf_op | source)
XLA Modules:
  0.0 117.9 jit_solution(6240497458659729511)
XLA Ops:
  0.6 0.8 copy.11
  1.4 0.1 reshape.13
  1.5 17.4 %first.1 = (f32[2,3,384,128]{3,2,1,0:T(8,128)S(1)}, s32[3,3,8,128]{3,2,1,0:T(8,128)S(1)}, bf16[256,256]{1,0:T(8,128)(2,1)S(1)}, bf16[256,256]{1,0:T(8,128)(2,1)S...) custom-call(f32[2,256,256]{2,1,0:T(8,128)} %obj_hbm.1, ...), custom_call_target="tpu_custom_call" | custom-call | tf_op jit(solution)/shard_map/first/pallas_call | solution.py:232
  18.9 26.2 %batch0.1 = (f32[2,3,384,128]{3,2,1,0:T(8,128)S(1)}, f32[9,128,128]{2,1,0:T(8,128)S(1)}) custom-call(s32[3,3,8,128]{3,2,1,0:T(8,128)S(1)} %get-tuple-element.16.offs, f32[2,3,384,128]{3,2,1,0:T(8,128)S(1)} %get-tuple-element.17.tiles, bf16[256,256]{1,0:T(8,128)(2,1)S(1)} %get-tuple-element.18.rest_0_, bf16[256,256]{1,0:T(8,128)(2,1)S(1)} %get-tuple-element.19.rest_1_, ...), custom_call_target="tpu_custom_call" | custom-call | tf_op jit(solution)/shard_map/batch0/pallas_call | solution.py:734
  45.1 25.1 %batch1.1 = (f32[2,3,384,128]{3,2,1,0:T(8,128)S(1)}, f32[9,128,128]{2,1,0:T(8,128)S(1)}) custom-call(s32[3,3,8,128]{3,2,1,0:T(8,128)S(1)} %get-tuple-element.16.offs, f32[2,3,384,128]{3,2,1,0:T(8,128)S(1)} %get-tuple-element.24.tiles, bf16[256,256]{1,0:T(8,128)(2,1)S(1)} %get-tuple-element.18.rest_0_, bf16[256,256]{1,0:T(8,128)(2,1)S(1)} %get-tuple-element.19.rest_1_, ...), custom_call_target="tpu_custom_call" | custom-call | tf_op jit(solution)/shard_map/batch1/pallas_call | solution.py:734
  70.2 46.1 %batch2.1 = (f32[2,256,256]{2,1,0:T(8,128)S(1)}, f32[128,8,128]{2,1,0:T(8,128)S(1)}) custom-call(s32[3,3,8,128]{3,2,1,0:T(8,128)S(1)} %get-tuple-element.16.offs, f32[2,3,384,128]{3,2,1,0:T(8,128)S(1)} %get-tuple-element.26.tiles, bf16[256,256]{1,0:T(8,128)(2,1)S(1)} %get-tuple-element.18.rest_0_, bf16[256,256]{1,0:T(8,128)(2,1)S(1)} %get-tuple-element.19.rest_1_, ...), custom_call_target="tpu_custom_call" | custom-call | tf_op jit(solution)/shard_map/batch2/pallas_call | solution.py:734
  116.3 0.8 copy.14
  117.1 0.8 copy.15
  (1 shorter events, 0.0 us)

commit v6 on v4

--- a/solution.py
+++ b/solution.py
@@ -146,8 +146,12 @@
     for c in loads:
         c.start()
     lane = lanes((TILE, N))
-    table[...] = jnp.full(table.shape, FAR, jnp.int32)
-    table[1, 1] = offs[...]
+    for cr in range(3):
+        for rr in range(3):
+            if (cr, rr) != (1, 1):
+                table[cr, rr] = jnp.full(table.shape[2:], FAR, jnp.int32)
+    own_offs = pltpu.make_async_copy(offs, table.at[1, 1], local.at[7])
+    own_offs.start()
     clear_missing([(left[0], hl), (right[0], hr),
                    (up[0], me.at[:, :, pl.ds(0, HALF), :]),
                    (down[0], me.at[:, :, pl.ds(PADROWS - HALF, HALF), :])])
@@ -158,6 +162,7 @@
         a, b = turn(obj[ch, :, 0:128]), turn(obj[ch, :, 128:256])
         me[1, ch, own] = jnp.where(lane < HALF, b, a)
         me[0, ch, own] = jnp.where(lane < HALF, a, b)
+    own_offs.wait()
     greeted((up, down, left, right))
 
     count = iter(range(100))
@@ -233,18 +238,18 @@
         first_kernel,
         out_shape=(
             jax.ShapeDtypeStruct((2, 3, PADROWS, N), f),
-            jax.ShapeDtypeStruct((3, 3, 8, N), jnp.int32),
+            jax.ShapeDtypeStruct((3, 3, BATCHES, 2, POS), jnp.int32),
         ) + tuple(jax.ShapeDtypeStruct(a.shape, a.dtype) for a in others),
-        in_specs=[hbm, VM] + [hbm] * 6,
+        in_specs=[hbm] * 8,
         out_specs=(VM,) * 8,
         scratch_shapes=[
             pltpu.VMEM((2, TILE, TILE), f),
             pltpu.VMEM((2, 2, PADROWS, N), f),
             strip, strip, strip, strip,
-            pltpu.VMEM((3, 3, 8, N), jnp.int32),
+            pltpu.VMEM((3, 3, BATCHES, 2, POS), jnp.int32),
             pltpu.SemaphoreType.DMA((14,)),
             pltpu.SemaphoreType.DMA((14,)),
-            pltpu.SemaphoreType.DMA((7,)),
+            pltpu.SemaphoreType.DMA((8,)),
         ],
         compiler_params=pltpu.CompilerParams(collective_id=0, has_side_effects=True, vmem_limit_bytes=14 * 2**20),
         name="first",
@@ -271,8 +276,8 @@
 
 def spot(offs, block, batch, p):
     cr, rr = block
-    r0 = offs[cr, rr, 0, batch * 8 + p * 2] + (rr - 1) * TILE + HALF
-    c0 = offs[cr, rr, 0, batch * 8 + p * 2 + 1] + (cr - 1) * TILE + HALF
+    r0 = offs[cr, rr, batch, 0, p] + (rr - 1) * TILE + HALF
+    c0 = offs[cr, rr, batch, 1, p] + (cr - 1) * TILE + HALF
     return r0, lax.shift_right_arithmetic(c0, 7), lax.bitwise_and(c0, 127)
 
 
@@ -403,29 +408,30 @@
 TILES = 144
 HALFT = 72
 PART = 36
-SPLITS = (("group", 8, 5, "x", 4, 2), ("x", 4, 9, "group", 8, 2))
+SPLITS = (("y", 4, 9, "x", 4, 3), ("x", 4, 9, "y", 4, 3))
 
 
 class Mates:
     def __init__(self):
         self.row, self.col = lax.axis_index("row"), lax.axis_index("col")
-        self.x, self.zh = self.row // 4, self.row % 4
-        self.core, self.group = self.col % 2, self.col // 2
+        self.x, self.y = self.row // 4, self.col // 4
+        self.z = self.row % 4 * 2 + self.col // 2 % 2
+        self.core = self.col % 2
         self.partner = {"row": self.row, "col": self.col + 1 - 2 * self.core}
 
     def at(self, axis, d):
-        if axis == "group":
-            k = lax.rem(self.group + d, 8)
-            return k, {"row": self.row, "col": k * 2 + self.core}
+        if axis == "y":
+            k = lax.rem(self.y + d, 4)
+            return k, {"row": self.row, "col": k * 4 + self.col % 4}
         if axis == "x":
             k = lax.rem(self.x + d, 4)
-            return k, {"row": k * 4 + self.zh, "col": self.col}
-        k = lax.rem(self.zh + d, 4)
-        return k, {"row": self.x * 4 + k, "col": self.col}
+            return k, {"row": k * 4 + self.row % 4, "col": self.col}
+        k = lax.rem(self.z + d, 8)
+        return k, {"row": self.x * 4 + k // 2, "col": self.y * 4 + k % 2 * 2 + self.core}
 
     def everyone(self):
-        return ([self.partner] + [self.at("group", d)[1] for d in range(1, 8)]
-                + [self.at("x", d)[1] for d in range(1, 4)] + [self.at("z", d)[1] for d in range(1, 4)])
+        return ([self.partner] + [self.at("y", d)[1] for d in range(1, 4)]
+                + [self.at("x", d)[1] for d in range(1, 4)] + [self.at("z", d)[1] for d in range(1, 8)])
 
 
 def reduce_part(part, mates, g, whole, bufs):
@@ -477,13 +483,13 @@
     cs = scatter(s2, r3, axis2, n2, p2)
     yield
     z[0] = collect(s2, r3, axis2, p2, cs)
-    cs = [go(z.at[0], z.at[d], mates.at("z", d)[1]) for d in range(1, 4)]
+    cs = [go(z.at[0], z.at[d], mates.at("z", d)[1]) for d in range(1, 8)]
     yield
     for c in cs:
         c.wait_recv()
-    acc = z[lax.rem(mates.zh, 4)]
-    for k in range(1, 4):
-        acc = acc + z[lax.rem(mates.zh - k + 4, 4)]
+    acc = z[lax.rem(mates.z, 8)]
+    for k in range(1, 8):
+        acc = acc + z[lax.rem(mates.z - k + 8, 8)]
     fin[...] = acc
     cs = gather(fin, ag1, axis2, n2, p2)
     yield
@@ -512,8 +518,8 @@
     refs = [shape(TILES)]
     for _, n1, p1, _, n2, p2 in SPLITS:
         refs += [shape(PART), shape(n1 * p1), shape(n1 - 1, p1), shape(n2 * p2), shape(n2 - 1, p2),
-                 shape(4, p2), shape(p2), shape(n2 * p2), shape(n1 * p1),
-                 pltpu.SemaphoreType.DMA((25,)), pltpu.SemaphoreType.DMA((25,))]
+                 shape(8, p2), shape(p2), shape(n2 * p2), shape(n1 * p1),
+                 pltpu.SemaphoreType.DMA((21,)), pltpu.SemaphoreType.DMA((21,))]
     return refs
 
 
@@ -524,7 +530,7 @@
         gin, *rest = rest
     others, parts = (), ()
     if last:
-        out, step_out, gout, flat, z, fixed, zl, light, ls, rs, ls_in, rs_in, me, fresh, from_up, from_down, send, recv, whole, *more = rest
+        fresh, whole_out, gout, flat, z, fixed, zl, light, ls, rs, ls_in, rs_in, me, from_up, from_down, send, recv, whole, *more = rest
         mates = Mates()
         others = mates.everyone()
         parts = [reduce_part(k, mates, flat, whole, more[k * PART_REFS:(k + 1) * PART_REFS]) for k in range(2)]
@@ -674,17 +680,9 @@
         update(0, HALF, HALF, from_up.at[0])
         row_links[0, True, 0].arrived()
         update(0, 256, HALF, from_down.at[0])
-        wide = lanes((TILE, N))
-        w = slice(HALF, HALF + TILE)
-        for ch in range(2):
-            m, e = fresh[0, ch, w], fresh[1, ch, w]
-            out[ch, :, 0:128] = turn(jnp.where(wide < HALF, m, e))
-            out[ch, :, 128:256] = turn(jnp.where(wide < HALF, e, m))
         for _ in range(4):
             advance()
-        inv = lax.rsqrt(whole[pl.ds(128, 16)] + PROBE_REG)
-        for k in range(8):
-            step_out[pl.ds(16 * k, 16)] = whole[pl.ds(16 * k, 16)] * inv
+        whole_out[...] = whole[...]
     else:
         for top, at in ((True, 0), (False, 64), (True, 64), (False, 0)):
             row_links[1, top, at].arrived()
@@ -710,7 +708,7 @@
     sums = jax.ShapeDtypeStruct((2 * MODES + 1, N, N), f)
     reach = HALF if last else N
     if last:
-        shapes = (jax.ShapeDtypeStruct((2, TILE, TILE), f), jax.ShapeDtypeStruct((128, 8, N), f))
+        shapes = (jax.ShapeDtypeStruct((2, 2, PADROWS, N), f), jax.ShapeDtypeStruct((TILES, 8, N), f))
         extra = [pltpu.VMEM((2 * MODES + 1, N, N), f), pltpu.VMEM((TILES, 8, N), f)]
     else:
         shapes = (jax.ShapeDtypeStruct((2, 3, PADROWS, N), f), sums)
@@ -727,7 +725,7 @@
             pltpu.VMEM((2, PADROWS, N), f),
             strip, strip, strip, strip,
             pltpu.VMEM((2, 2, PADROWS, N), f),
-            pltpu.VMEM((2, 2, PADROWS, N), f),
+        ] + ([] if last else [pltpu.VMEM((2, 2, PADROWS, N), f)]) + [
             pltpu.VMEM((2, 2, reach, N), f),
             pltpu.VMEM((2, 2, reach, N), f),
         ] + ([] if last else [strip] * 4) + [
@@ -740,17 +738,40 @@
     )(offs, tiles, *others, *gin)
 
 
+def final_kernel(fresh, whole, out, step_out):
+    wide = lanes((TILE, N))
+    w = slice(HALF, HALF + TILE)
+    for ch in range(2):
+        m, e = fresh[0, ch, w], fresh[1, ch, w]
+        out[ch, :, 0:128] = turn(jnp.where(wide < HALF, m, e))
+        out[ch, :, 128:256] = turn(jnp.where(wide < HALF, e, m))
+    inv = lax.rsqrt(whole[pl.ds(128, 16)] + PROBE_REG)
+    for k in range(8):
+        step_out[pl.ds(16 * k, 16)] = whole[pl.ds(16 * k, 16)] * inv
+
+
+def run_final(fresh, whole):
+    return pl.pallas_call(
+        final_kernel,
+        out_shape=(jax.ShapeDtypeStruct((2, TILE, TILE), jnp.float32), jax.ShapeDtypeStruct((128, 8, N), jnp.float32)),
+        in_specs=[VM, VM],
+        out_specs=(VM, VM),
+        compiler_params=pltpu.CompilerParams(vmem_limit_bytes=8 * 2**20),
+        name="final",
+    )(fresh, whole)
+
+
 def on_device(object_field, probe, amplitudes, offsets):
-    mine = jnp.pad(offsets.reshape(1, 24), ((0, 7), (0, N - 24)))
+    mine = jnp.swapaxes(offsets, 3, 4).reshape(BATCHES, 2, POS)
     amps = amplitudes.reshape(BATCHES, POS, N, N)
     tabs = [jnp.asarray(t) for t in tables()]
     keep = lambda a: pltpu.with_memory_space_constraint(a, pltpu.HBM)
-    tiles, offs, *others = run_first(keep(object_field), mine, [keep(a) for a in (*tabs, amps, probe)])
+    tiles, offs, *others = run_first(keep(object_field), keep(mine), [keep(a) for a in (*tabs, amps, probe)])
     grads = ()
     for b in range(BATCHES - 1):
         tiles, sums = run_batch(b, False, offs, tiles, others, grads)
         grads = (sums,)
-    obj, step = run_batch(BATCHES - 1, True, offs, tiles, others, grads)
+    obj, step = run_final(*run_batch(BATCHES - 1, True, offs, tiles, others, grads))
     return obj, step.reshape(2, MODES, N, N)
 
 

time: 117 us -> 114 us (0.974)
  local copies, waits for them, and re-layouts: 2.47 us -> 0 us
    unnamed x3 -> x0, local copies, waits for them, and re-layouts: 2.37 us -> none
    pallas_call x3, Pallas kernels: 96.7 us -> 94.7 us  [run_batch(): pl.pallas_call(functools.partial(batch_kernel, batch, last), out_shape=sh...]
where the time goes in v6:
time: 114 us
  Pallas kernels  113 us (99%)
    pallas_call x3, Pallas kernels, run_batch(): pl.pallas_call(functools.partial(batch_kernel, batch, last), out_shape=sh...  94.7 us
    pallas_call x1, Pallas kernels, run_first(): pl.pallas_call(first_kernel, out_shape=(jax.ShapeDtypeStruct((2, 3, PADRO...  17.4 us

profile of v6, /device:TPU:1, one launch (start us, length us, event | category | flops | bytes accessed | tf_op | source)
XLA Modules:
  0.0 113.8 jit_solution(7714606495254017573)
XLA Ops:
  0.6 17.4 %first.1 = (f32[2,3,384,128]{3,2,1,0:T(8,128)S(1)}, s32[3,3,3,2,4]{4,3,2,1,0:T(2,128)S(1)}, bf16[256,256]{1,0:T(8,128)(2,1)S(1)}, bf16[256,256]{1,0:T(8,128)(2,1...) custom-call(f32[2,256,256]{2,1,0:T(8,128)} %obj_hbm.1, ...), custom_call_target="tpu_custom_call" | custom-call | tf_op jit(solution)/shard_map/first/pallas_call | solution.py:237
  18.0 26.7 %batch0.1 = (f32[2,3,384,128]{3,2,1,0:T(8,128)S(1)}, f32[9,128,128]{2,1,0:T(8,128)S(1)}) custom-call(s32[3,3,3,2,4]{4,3,2,1,0:T(2,128)S(1)} %get-tuple-element.18.offs, f32[2,3,384,128]{3,2,1,0:T(8,128)S(1)} %get-tuple-element.19.tiles, bf16[256,256]{1,0:T(8,128)(2,1)S(1)} %get-tuple-element.20.rest_0_, bf16[256,256]{1,0:T(8,128)(2,1)S(1)} %get-tuple-element.21.rest_1_, ...), custom_call_target="tpu_custom_call" | custom-call | tf_op jit(solution)/shard_map/batch0/pallas_call | solution.py:716
  44.8 24.2 %batch1.1 = (f32[2,3,384,128]{3,2,1,0:T(8,128)S(1)}, f32[9,128,128]{2,1,0:T(8,128)S(1)}) custom-call(s32[3,3,3,2,4]{4,3,2,1,0:T(2,128)S(1)} %get-tuple-element.18.offs, f32[2,3,384,128]{3,2,1,0:T(8,128)S(1)} %get-tuple-element.26.tiles, bf16[256,256]{1,0:T(8,128)(2,1)S(1)} %get-tuple-element.20.rest_0_, bf16[256,256]{1,0:T(8,128)(2,1)S(1)} %get-tuple-element.21.rest_1_, ...), custom_call_target="tpu_custom_call" | custom-call | tf_op jit(solution)/shard_map/batch1/pallas_call | solution.py:716
  69.0 43.7 %batch2.1 = (f32[2,2,384,128]{3,2,1,0:T(8,128)S(1)}, f32[144,8,128]{2,1,0:T(8,128)S(1)}) custom-call(s32[3,3,3,2,4]{4,3,2,1,0:T(2,128)S(1)} %get-tuple-element.18.offs, f32[2,3,384,128]{3,2,1,0:T(8,128)S(1)} %get-tuple-element.28.tiles, bf16[256,256]{1,0:T(8,128)(2,1)S(1)} %get-tuple-element.20.rest_0_, bf16[256,256]{1,0:T(8,128)(2,1)S(1)} %get-tuple-element.21.rest_1_, ...), custom_call_target="tpu_custom_call" | custom-call | tf_op jit(solution)/shard_map/batch2/pallas_call | solution.py:716
  112.7 1.1 %final.1 = (f32[2,256,256]{2,1,0:T(8,128)}, f32[128,8,128]{2,1,0:T(8,128)}) custom-call(f32[2,2,384,128]{3,2,1,0:T(8,128)S(1)} %get-tuple-element.30.fresh, f32[144,8,128]{2,1,0:T(8,128)S(1)} %get-tuple-element.31.whole), custom_call_target="tpu_custom_call" | custom-call | tf_op jit(solution)/shard_map/final/pallas_call | solution.py:754

commit v7 on v6

--- a/solution.py
+++ b/solution.py
@@ -405,10 +405,10 @@
         light[j] = jnp.where(inside, 1.0 / (light[j] + OBJECT_REG), 0.0)
 
 
-TILES = 144
-HALFT = 72
-PART = 36
-SPLITS = (("y", 4, 9, "x", 4, 3), ("x", 4, 9, "y", 4, 3))
+ROWS = 1152
+HALFT = 576
+PART = 288
+SPLITS = (("y", 4, 72, "x", 4, 18), ("x", 4, 72, "y", 4, 18))
 
 
 class Mates:
@@ -470,9 +470,6 @@
         return cs
 
     core = mates.core
-    if s1.shape[0] > PART:
-        s1[pl.ds(PART, s1.shape[0] - PART)] = jnp.zeros((s1.shape[0] - PART, 8, N), jnp.float32)
-    s2[pl.ds(p1, s2.shape[0] - p1)] = jnp.zeros((s2.shape[0] - p1, 8, N), jnp.float32)
     c = go(g.at[pl.ds((1 - core) * HALFT + part * PART, PART)], r1, mates.partner)
     yield
     c.wait_recv()
@@ -514,8 +511,8 @@
 
 def reduction_scratch():
     f = jnp.float32
-    shape = lambda *n: pltpu.VMEM(n + (8, N), f)
-    refs = [shape(TILES)]
+    shape = lambda *n: pltpu.VMEM(n + (N,), f)
+    refs = [shape(ROWS)]
     for _, n1, p1, _, n2, p2 in SPLITS:
         refs += [shape(PART), shape(n1 * p1), shape(n1 - 1, p1), shape(n2 * p2), shape(n2 - 1, p2),
                  shape(8, p2), shape(p2), shape(n2 * p2), shape(n1 * p1),
@@ -617,16 +614,20 @@
         me[1, 0, w] += jnp.where(side < HALF, a, turn(b))
         me[1, 1, w] += jnp.where(side < HALF, turn(a), b)
 
+    if last:
+        static_terms(batch, tiles, probe, amp, gout, fixed, tabs)
+        flat[...] = gout[...].reshape(ROWS, N)
+        advance()
     middle(0)
     send_rows(0, True, 0, reach)
     middle(2)
     send_rows(0, False, PADROWS - reach, reach)
+    if last:
+        advance()
     side_strips(1)
     send_cols(N, N)
-    static_terms(batch, tiles, probe, amp, gout, fixed, tabs)
-    if last:
-        flat[...] = gout[...].reshape(TILES, 8, N)
-    advance()
+    if not last:
+        static_terms(batch, tiles, probe, amp, gout, fixed, tabs)
     order = ((0, True), (320, False), (64, True), (256, False))
     for i in (0, 2):
         side_strips(i)
@@ -635,7 +636,6 @@
     send_cols(320, HALF)
     send_cols(64, HALF)
     send_cols(256, HALF)
-    advance()
     middle(1)
     light_maps(batch, offs, probe, zl, light)
     for at, top in order:
@@ -708,8 +708,8 @@
     sums = jax.ShapeDtypeStruct((2 * MODES + 1, N, N), f)
     reach = HALF if last else N
     if last:
-        shapes = (jax.ShapeDtypeStruct((2, 2, PADROWS, N), f), jax.ShapeDtypeStruct((TILES, 8, N), f))
-        extra = [pltpu.VMEM((2 * MODES + 1, N, N), f), pltpu.VMEM((TILES, 8, N), f)]
+        shapes = (jax.ShapeDtypeStruct((2, 2, PADROWS, N), f), jax.ShapeDtypeStruct((ROWS, N), f))
+        extra = [pltpu.VMEM((2 * MODES + 1, N, N), f), pltpu.VMEM((ROWS, N), f)]
     else:
         shapes = (jax.ShapeDtypeStruct((2, 3, PADROWS, N), f), sums)
         extra = []
@@ -745,15 +745,15 @@
         m, e = fresh[0, ch, w], fresh[1, ch, w]
         out[ch, :, 0:128] = turn(jnp.where(wide < HALF, m, e))
         out[ch, :, 128:256] = turn(jnp.where(wide < HALF, e, m))
-    inv = lax.rsqrt(whole[pl.ds(128, 16)] + PROBE_REG)
-    for k in range(8):
-        step_out[pl.ds(16 * k, 16)] = whole[pl.ds(16 * k, 16)] * inv
+    inv = lax.rsqrt(whole[pl.ds(2 * MODES * N, N)] + PROBE_REG)
+    for k in range(2 * MODES):
+        step_out[pl.ds(N * k, N)] = whole[pl.ds(N * k, N)] * inv
 
 
 def run_final(fresh, whole):
     return pl.pallas_call(
         final_kernel,
-        out_shape=(jax.ShapeDtypeStruct((2, TILE, TILE), jnp.float32), jax.ShapeDtypeStruct((128, 8, N), jnp.float32)),
+        out_shape=(jax.ShapeDtypeStruct((2, TILE, TILE), jnp.float32), jax.ShapeDtypeStruct((2 * MODES * N, N), jnp.float32)),
         in_specs=[VM, VM],
         out_specs=(VM, VM),
         compiler_params=pltpu.CompilerParams(vmem_limit_bytes=8 * 2**20),

time: 114 us -> 117 us (1.026)
  Pallas kernels: 113 us -> 116 us
    pallas_call x3, Pallas kernels: 94.7 us -> 97.4 us  [run_batch(): pl.pallas_call(functools.partial(batch_kernel, batch, last), out_shape=sh...]
where the time goes in v7:
time: 117 us
  Pallas kernels  116 us (99%)
    pallas_call x3, Pallas kernels, run_batch(): pl.pallas_call(functools.partial(batch_kernel, batch, last), out_shape=sh...  97.4 us
    pallas_call x1, Pallas kernels, run_first(): pl.pallas_call(first_kernel, out_shape=(jax.ShapeDtypeStruct((2, 3, PADRO...  17.4 us

profile of v7, /device:TPU:1, one launch (start us, length us, event | category | flops | bytes accessed | tf_op | source)
XLA Modules:
  0.0 116.5 jit_solution(426226943261533332)
XLA Ops:
  0.6 17.4 %first.1 = (f32[2,3,384,128]{3,2,1,0:T(8,128)S(1)}, s32[3,3,3,2,4]{4,3,2,1,0:T(2,128)S(1)}, bf16[256,256]{1,0:T(8,128)(2,1)S(1)}, bf16[256,256]{1,0:T(8,128)(2,1...) custom-call(f32[2,256,256]{2,1,0:T(8,128)} %obj_hbm.1, ...), custom_call_target="tpu_custom_call" | custom-call | tf_op jit(solution)/shard_map/first/pallas_call | solution.py:237
  18.0 26.8 %batch0.1 = (f32[2,3,384,128]{3,2,1,0:T(8,128)S(1)}, f32[9,128,128]{2,1,0:T(8,128)S(1)}) custom-call(s32[3,3,3,2,4]{4,3,2,1,0:T(2,128)S(1)} %get-tuple-element.18.offs, f32[2,3,384,128]{3,2,1,0:T(8,128)S(1)} %get-tuple-element.19.tiles, bf16[256,256]{1,0:T(8,128)(2,1)S(1)} %get-tuple-element.20.rest_0_, bf16[256,256]{1,0:T(8,128)(2,1)S(1)} %get-tuple-element.21.rest_1_, ...), custom_call_target="tpu_custom_call" | custom-call | tf_op jit(solution)/shard_map/batch0/pallas_call | solution.py:716
  44.8 23.8 %batch1.1 = (f32[2,3,384,128]{3,2,1,0:T(8,128)S(1)}, f32[9,128,128]{2,1,0:T(8,128)S(1)}) custom-call(s32[3,3,3,2,4]{4,3,2,1,0:T(2,128)S(1)} %get-tuple-element.18.offs, f32[2,3,384,128]{3,2,1,0:T(8,128)S(1)} %get-tuple-element.26.tiles, bf16[256,256]{1,0:T(8,128)(2,1)S(1)} %get-tuple-element.20.rest_0_, bf16[256,256]{1,0:T(8,128)(2,1)S(1)} %get-tuple-element.21.rest_1_, ...), custom_call_target="tpu_custom_call" | custom-call | tf_op jit(solution)/shard_map/batch1/pallas_call | solution.py:716
  68.5 46.9 %batch2.1 = (f32[2,2,384,128]{3,2,1,0:T(8,128)S(1)}, f32[1152,128]{1,0:T(8,128)S(1)}) custom-call(s32[3,3,3,2,4]{4,3,2,1,0:T(2,128)S(1)} %get-tuple-element.18.offs, f32[2,3,384,128]{3,2,1,0:T(8,128)S(1)} %get-tuple-element.28.tiles, bf16[256,256]{1,0:T(8,128)(2,1)S(1)} %get-tuple-element.20.rest_0_, bf16[256,256]{1,0:T(8,128)(2,1)S(1)} %get-tuple-element.21.rest_1_, ...), custom_call_target="tpu_custom_call" | custom-call | tf_op jit(solution)/shard_map/batch2/pallas_call | solution.py:716
  115.4 1.1 final.1

commit v8 on v7

--- a/solution.py
+++ b/solution.py
@@ -614,20 +614,16 @@
         me[1, 0, w] += jnp.where(side < HALF, a, turn(b))
         me[1, 1, w] += jnp.where(side < HALF, turn(a), b)
 
-    if last:
-        static_terms(batch, tiles, probe, amp, gout, fixed, tabs)
-        flat[...] = gout[...].reshape(ROWS, N)
-        advance()
     middle(0)
     send_rows(0, True, 0, reach)
     middle(2)
     send_rows(0, False, PADROWS - reach, reach)
-    if last:
-        advance()
     side_strips(1)
     send_cols(N, N)
-    if not last:
-        static_terms(batch, tiles, probe, amp, gout, fixed, tabs)
+    static_terms(batch, tiles, probe, amp, gout, fixed, tabs)
+    if last:
+        flat[...] = gout[...].reshape(ROWS, N)
+    advance()
     order = ((0, True), (320, False), (64, True), (256, False))
     for i in (0, 2):
         side_strips(i)
@@ -636,13 +632,18 @@
     send_cols(320, HALF)
     send_cols(64, HALF)
     send_cols(256, HALF)
+    advance()
     middle(1)
-    light_maps(batch, offs, probe, zl, light)
-    for at, top in order:
+    if not last:
+        light_maps(batch, offs, probe, zl, light)
+    for at, top in order[:2] if last else order:
         fold_cols(at, HALF)
-        if not last or at in (0, 320):
-            send_rows(1, top, at, HALF)
+        send_rows(1, top, at, HALF)
     advance()
+    if last:
+        light_maps(batch, offs, probe, zl, light)
+        for at, top in order[2:]:
+            fold_cols(at, HALF)
     fold_cols(N, N)
     halos = []
 

time: 117 us -> 112 us (0.957)
  Pallas kernels: 116 us -> 111 us
    pallas_call x3, Pallas kernels: 97.4 us -> 92.9 us  [run_batch(): pl.pallas_call(functools.partial(batch_kernel, batch, last), out_shape=sh...]
where the time goes in v8:
time: 112 us
  Pallas kernels  111 us (99%)
    pallas_call x3, Pallas kernels, run_batch(): pl.pallas_call(functools.partial(batch_kernel, batch, last), out_shape=sh...  92.9 us
    pallas_call x1, Pallas kernels, run_first(): pl.pallas_call(first_kernel, out_shape=(jax.ShapeDtypeStruct((2, 3, PADRO...  17.4 us

profile of v8, /device:TPU:1, one launch (start us, length us, event | category | flops | bytes accessed | tf_op | source)
XLA Modules:
  0.0 112.1 jit_solution(9811026592293266825)
XLA Ops:
  0.6 17.4 %first.1 = (f32[2,3,384,128]{3,2,1,0:T(8,128)S(1)}, s32[3,3,3,2,4]{4,3,2,1,0:T(2,128)S(1)}, bf16[256,256]{1,0:T(8,128)(2,1)S(1)}, bf16[256,256]{1,0:T(8,128)(2,1...) custom-call(f32[2,256,256]{2,1,0:T(8,128)} %obj_hbm.1, ...), custom_call_target="tpu_custom_call" | custom-call | tf_op jit(solution)/shard_map/first/pallas_call | solution.py:237
  18.0 26.7 %batch0.1 = (f32[2,3,384,128]{3,2,1,0:T(8,128)S(1)}, f32[9,128,128]{2,1,0:T(8,128)S(1)}) custom-call(s32[3,3,3,2,4]{4,3,2,1,0:T(2,128)S(1)} %get-tuple-element.18.offs, f32[2,3,384,128]{3,2,1,0:T(8,128)S(1)} %get-tuple-element.19.tiles, bf16[256,256]{1,0:T(8,128)(2,1)S(1)} %get-tuple-element.20.rest_0_, bf16[256,256]{1,0:T(8,128)(2,1)S(1)} %get-tuple-element.21.rest_1_, ...), custom_call_target="tpu_custom_call" | custom-call | tf_op jit(solution)/shard_map/batch0/pallas_call | solution.py:717
  44.8 24.9 %batch1.1 = (f32[2,3,384,128]{3,2,1,0:T(8,128)S(1)}, f32[9,128,128]{2,1,0:T(8,128)S(1)}) custom-call(s32[3,3,3,2,4]{4,3,2,1,0:T(2,128)S(1)} %get-tuple-element.18.offs, f32[2,3,384,128]{3,2,1,0:T(8,128)S(1)} %get-tuple-element.26.tiles, bf16[256,256]{1,0:T(8,128)(2,1)S(1)} %get-tuple-element.20.rest_0_, bf16[256,256]{1,0:T(8,128)(2,1)S(1)} %get-tuple-element.21.rest_1_, ...), custom_call_target="tpu_custom_call" | custom-call | tf_op jit(solution)/shard_map/batch1/pallas_call | solution.py:717
  69.7 41.2 %batch2.1 = (f32[2,2,384,128]{3,2,1,0:T(8,128)S(1)}, f32[1152,128]{1,0:T(8,128)S(1)}) custom-call(s32[3,3,3,2,4]{4,3,2,1,0:T(2,128)S(1)} %get-tuple-element.18.offs, f32[2,3,384,128]{3,2,1,0:T(8,128)S(1)} %get-tuple-element.28.tiles, bf16[256,256]{1,0:T(8,128)(2,1)S(1)} %get-tuple-element.20.rest_0_, bf16[256,256]{1,0:T(8,128)(2,1)S(1)} %get-tuple-element.21.rest_1_, ...), custom_call_target="tpu_custom_call" | custom-call | tf_op jit(solution)/shard_map/batch2/pallas_call | solution.py:717
  111.0 1.1 %final.1 = (f32[2,256,256]{2,1,0:T(8,128)}, f32[1024,128]{1,0:T(8,128)}) custom-call(f32[2,2,384,128]{3,2,1,0:T(8,128)S(1)} %get-tuple-element.30.fresh, f32[1152,128]{1,0:T(8,128)S(1)} %get-tuple-element.31.whole), custom_call_target="tpu_custom_call" | custom-call | tf_op jit(solution)/shard_map/final/pallas_call | solution.py:755

commit v9 on v8

--- a/solution.py
+++ b/solution.py
@@ -634,14 +634,12 @@
     send_cols(256, HALF)
     advance()
     middle(1)
-    if not last:
-        light_maps(batch, offs, probe, zl, light)
     for at, top in order[:2] if last else order:
         fold_cols(at, HALF)
         send_rows(1, top, at, HALF)
     advance()
+    light_maps(batch, offs, probe, zl, light)
     if last:
-        light_maps(batch, offs, probe, zl, light)
         for at, top in order[2:]:
             fold_cols(at, HALF)
     fold_cols(N, N)

time: 112 us -> 112 us (level)
  no operation moved by 1% of the time
where the time goes in v9:
time: 112 us
  Pallas kernels  111 us (99%)
    pallas_call x3, Pallas kernels, run_batch(): pl.pallas_call(functools.partial(batch_kernel, batch, last), out_shape=sh...  92.9 us
    pallas_call x1, Pallas kernels, run_first(): pl.pallas_call(first_kernel, out_shape=(jax.ShapeDtypeStruct((2, 3, PADRO...  17.4 us

profile of v9, /device:TPU:1, one launch (start us, length us, event | category | flops | bytes accessed | tf_op | source)
XLA Modules:
  0.0 112.1 jit_solution(16912818572581653253)
XLA Ops:
  0.6 17.4 %first.1 = (f32[2,3,384,128]{3,2,1,0:T(8,128)S(1)}, s32[3,3,3,2,4]{4,3,2,1,0:T(2,128)S(1)}, bf16[256,256]{1,0:T(8,128)(2,1)S(1)}, bf16[256,256]{1,0:T(8,128)(2,1...) custom-call(f32[2,256,256]{2,1,0:T(8,128)} %obj_hbm.1, ...), custom_call_target="tpu_custom_call" | custom-call | tf_op jit(solution)/shard_map/first/pallas_call | solution.py:237
  18.0 26.8 %batch0.1 = (f32[2,3,384,128]{3,2,1,0:T(8,128)S(1)}, f32[9,128,128]{2,1,0:T(8,128)S(1)}) custom-call(s32[3,3,3,2,4]{4,3,2,1,0:T(2,128)S(1)} %get-tuple-element.18.offs, f32[2,3,384,128]{3,2,1,0:T(8,128)S(1)} %get-tuple-element.19.tiles, bf16[256,256]{1,0:T(8,128)(2,1)S(1)} %get-tuple-element.20.rest_0_, bf16[256,256]{1,0:T(8,128)(2,1)S(1)} %get-tuple-element.21.rest_1_, ...), custom_call_target="tpu_custom_call" | custom-call | tf_op jit(solution)/shard_map/batch0/pallas_call | solution.py:715
  44.8 24.9 %batch1.1 = (f32[2,3,384,128]{3,2,1,0:T(8,128)S(1)}, f32[9,128,128]{2,1,0:T(8,128)S(1)}) custom-call(s32[3,3,3,2,4]{4,3,2,1,0:T(2,128)S(1)} %get-tuple-element.18.offs, f32[2,3,384,128]{3,2,1,0:T(8,128)S(1)} %get-tuple-element.26.tiles, bf16[256,256]{1,0:T(8,128)(2,1)S(1)} %get-tuple-element.20.rest_0_, bf16[256,256]{1,0:T(8,128)(2,1)S(1)} %get-tuple-element.21.rest_1_, ...), custom_call_target="tpu_custom_call" | custom-call | tf_op jit(solution)/shard_map/batch1/pallas_call | solution.py:715
  69.7 41.2 %batch2.1 = (f32[2,2,384,128]{3,2,1,0:T(8,128)S(1)}, f32[1152,128]{1,0:T(8,128)S(1)}) custom-call(s32[3,3,3,2,4]{4,3,2,1,0:T(2,128)S(1)} %get-tuple-element.18.offs, f32[2,3,384,128]{3,2,1,0:T(8,128)S(1)} %get-tuple-element.28.tiles, bf16[256,256]{1,0:T(8,128)(2,1)S(1)} %get-tuple-element.20.rest_0_, bf16[256,256]{1,0:T(8,128)(2,1)S(1)} %get-tuple-element.21.rest_1_, ...), custom_call_target="tpu_custom_call" | custom-call | tf_op jit(solution)/shard_map/batch2/pallas_call | solution.py:715
  111.0 1.1 %final.1 = (f32[2,256,256]{2,1,0:T(8,128)}, f32[1024,128]{1,0:T(8,128)}) custom-call(f32[2,2,384,128]{3,2,1,0:T(8,128)S(1)} %get-tuple-element.30.fresh, f32[1152,128]{1,0:T(8,128)S(1)} %get-tuple-element.31.whole), custom_call_target="tpu_custom_call" | custom-call | tf_op jit(solution)/shard_map/final/pallas_call | solution.py:753
